TPU v7x, 32 devices: a whole 2x2x4 slice. The times are simulated.
32 devices in a mesh: dp: 8 (over y, x, core), seq: 4 (over z).
Axes of the slice: x: 2, y: 2, z: 4, core: 2. Of those that a mesh axis runs over, the one named last changes fastest.
Arguments:
- tokens: bfloat16 [2, 8, 1024, 768], P(None, 'dp', 'seq'), may hold values from -6 to 6
- lengths: int32 [2, 8], P(None, 'dp'), may hold values from 256 to 1024, as said below
- dealing: int32 [2, 8], P(None, 'dp'), may hold values from 0 to 7, each once within a row
- cotangent: bfloat16 [2, 8, 1024, 768], P(None, 'dp', 'seq'), may hold values from -6 to 6
- in_weight: bfloat16 [768, 3352], P(('dp', 'seq')), may hold values from -0.21875 to 0.21875
- out_weight: bfloat16 [1536, 768], P(('dp', 'seq')), may hold values from -0.15625 to 0.15625
- norm_gain: bfloat16 [768], P(('dp', 'seq')), may hold values from 0.5 to 1.5
- gate_gain: bfloat16 [1536], P(('dp', 'seq')), may hold values from 0.5 to 1.5
- conv_weight: float32 [4, 1792], replicated, may hold values from -3 to 3
- conv_bias: float32 [1792], replicated, may hold values from -0.5 to 0.5
- decay_log: float32 [24], replicated, may hold values from -5 to 1
- step_bias: float32 [24], replicated, may hold values from -4 to -2
- skip_gain: float32 [24], replicated, may hold values from 0.5 to 1.5
Outputs:
- outputs: bfloat16 [2, 8, 1024, 768], P(None, 'dp', 'seq')
- grad_tokens: bfloat16 [2, 8, 1024, 768], P(None, 'dp', 'seq')
- grad_in_weight: float32 [768, 3352], P(('dp', 'seq'))
- grad_out_weight: float32 [1536, 768], P(('dp', 'seq'))
- grad_norm_gain: float32 [768], P(('dp', 'seq'))
- grad_gate_gain: float32 [1536], P(('dp', 'seq'))
- grad_conv_weight: float32 [4, 1792], replicated
- grad_conv_bias: float32 [1792], replicated
- grad_decay_log: float32 [24], replicated
- grad_step_bias: float32 [24], replicated
- grad_skip_gain: float32 [24], replicated
Inputs may be any that keep to these rules, and one draw needn't show every extreme that they name: `lengths`: in every draw one sequence has exactly 1024 valid tokens and one exactly 256. Each row of dealing names every slot of its micro-batch once.
All inputs are finite; a program needn't handle non-finite values.
Results may differ from a plain program's by a relative error of at most 0.0075.
Values may be sent and summed in bfloat16 or wider, within the bound.
No kernel may reach another device: no remote copies, remote signals or barrier semaphores. Data moves between devices by JAX's collectives and lax.ppermute only.
A program may use at most 192 MiB of HBM per device.

v0:
```python
import jax
import jax.numpy as jnp
from jax import lax
from jax.sharding import PartitionSpec as P

INNER = 1536
HEADS = 24
HDIM = 64
STATE = 128
KCONV = 4


EPSILON = 1e-05
PRECISE = lax.Precision.HIGHEST
WIDE_TYPE = jnp.float32
NARROW_TYPE = jnp.bfloat16


def as_sent(x):

    def short(part):
        return part.astype(jnp.bfloat16) if part.dtype == jnp.float32 else part

    return jax.tree.map(short, x)


def swapped(value, axis, apart):
    mask = 2**apart
    pairs = [(source, source ^ mask) for source in range(lax.axis_size(axis))]
    return lax.ppermute(value, axis, pairs)


def from_behind(block, axis, distance):
    devices = range(lax.axis_size(axis))
    route = [(i - distance, i) for i in devices if i - distance in devices]
    return lax.ppermute(block, axis, route)


def norm_rows(values, gain_row):
    return (
        values * lax.rsqrt(jnp.mean(values * values, axis=-1, keepdims=True) + EPSILON) * gain_row
    )


def gated_norm(values, gate_in, gain_row):
    return norm_rows(values * jax.nn.silu(gate_in), gain_row)


def take_partner(dp_index, level, stride_bit, own_keys, other_keys):
    ascending = dp_index // 2**level % 2 == 0
    lower_side = dp_index // 2**stride_bit % 2 == 0
    keep_small = ascending == lower_side
    return jnp.where(keep_small, other_keys < own_keys, other_keys > own_keys)


def pick_rows(taken, other, own):
    shape = taken.shape + (1,) * (own.ndim - 1)
    return jnp.where(taken.reshape(shape), other, own)


def deal_sequences(tokens, lengths, dealing):
    dp_index = lax.axis_index("dp")
    levels = lax.axis_size("dp").bit_length() - 1
    own_keys = dealing[:, 0]
    length_list = lengths[:, 0]
    anchor = jnp.zeros_like(own_keys) + dp_index
    moved = tokens
    for level in range(1, levels + 1):
        for stride_bit in range(level - 1, -1, -1):
            other = (
                swapped(moved, "dp", stride_bit),
                swapped(as_sent(length_list), "dp", stride_bit).astype(length_list.dtype),
                swapped(as_sent(anchor), "dp", stride_bit).astype(anchor.dtype),
                swapped(as_sent(own_keys), "dp", stride_bit).astype(own_keys.dtype),
            )
            taken = take_partner(dp_index, level, stride_bit, own_keys, other[3])
            moved = pick_rows(taken, other[0], moved)
            length_list = pick_rows(taken, other[1], length_list)
            anchor = pick_rows(taken, other[2], anchor)
            own_keys = pick_rows(taken, other[3], own_keys)
    return (moved, length_list, anchor)


def return_sequences(grads, anchor):
    dp_index = lax.axis_index("dp")
    levels = lax.axis_size("dp").bit_length() - 1
    own_keys = anchor
    moved = grads
    for level in range(1, levels + 1):
        for stride_bit in range(level - 1, -1, -1):
            other = (
                swapped(moved, "dp", stride_bit),
                swapped(as_sent(own_keys), "dp", stride_bit).astype(own_keys.dtype),
            )
            taken = take_partner(dp_index, level, stride_bit, own_keys, other[1])
            moved = pick_rows(taken, other[0], moved)
            own_keys = pick_rows(taken, other[1], own_keys)
    return moved


def segment_of(cumulative, block_len):
    causal = (jnp.arange(block_len)[:, None] >= jnp.arange(block_len)[None, :])[None, :, :, None]
    spread_diff = cumulative[:, :, None, :] - cumulative[:, None, :, :]
    return jnp.where(causal, jnp.exp(jnp.where(causal, spread_diff, 0.0)), 0.0)


def forward_micro(tok, length_one, full, small):
    in_full, out_full, norm_full, gate_full = full
    conv_weight, conv_bias, decay_log, step_bias, skip_gain = small
    block_len = tok.shape[1]
    channels = INNER + 2 * STATE
    inputs_f = tok.astype(WIDE_TYPE)
    normed_f, norm_back = jax.vjp(norm_rows, inputs_f, norm_full.astype(WIDE_TYPE))
    normed = normed_f.astype(NARROW_TYPE)
    projected = jnp.einsum("bcd,dk->bck", normed, in_full, preferred_element_type=WIDE_TYPE)
    gate_in = projected[..., :INNER]
    conv_in = projected[..., INNER : INNER + channels]
    step_raw = projected[..., INNER + channels :]
    tail_rows = conv_in[:, block_len - (KCONV - 1) :]
    before = from_behind(tail_rows, "seq", 1)
    extended = jnp.concatenate([before, conv_in], axis=1)
    conv_out = conv_bias + conv_weight[0] * extended[:, 0:block_len]
    for offset in range(1, KCONV):
        conv_out = conv_out + conv_weight[offset] * extended[:, offset : offset + block_len]
    activated = jax.nn.silu(conv_out)
    values = activated[..., :INNER].astype(NARROW_TYPE).reshape(1, block_len, HEADS, HDIM)
    in_keys = activated[..., INNER : INNER + STATE].astype(NARROW_TYPE)
    out_keys = activated[..., INNER + STATE :].astype(NARROW_TYPE)
    values_f = values.astype(WIDE_TYPE)
    in_keys_f = in_keys.astype(WIDE_TYPE)
    out_keys_f = out_keys.astype(WIDE_TYPE)
    position = lax.axis_index("seq") * block_len + jnp.arange(block_len, dtype=jnp.int32)
    valid_mask = (position[None, :] < length_one[:, None]).astype(WIDE_TYPE)
    step_pre = step_raw + step_bias
    step_size = jax.nn.softplus(step_pre) * valid_mask[..., None]
    decay_rates = jnp.exp(decay_log)
    log_decay = -decay_rates * step_size
    cumulative = jnp.cumsum(log_decay, axis=1)
    segment = segment_of(cumulative, block_len)
    affinity = jnp.einsum("btn,bsn->bts", out_keys, in_keys, preferred_element_type=WIDE_TYPE)
    mixing = (affinity[..., None] * segment * step_size[:, None, :, :]).astype(NARROW_TYPE)
    local_part = jnp.einsum("btsh,bshp->bthp", mixing, values, preferred_element_type=WIDE_TYPE)
    last_decay = cumulative[:, -1:, :]
    tail_decay = jnp.exp(last_decay - cumulative)
    weights_in = tail_decay * step_size
    weighted = weights_in[..., None] * values_f
    update = jnp.einsum("bthp,btn->bhpn", weighted, in_keys_f, precision=PRECISE)
    total_decay = jnp.exp(last_decay[:, 0, :])

    def relay_step(iteration, carried):
        return from_behind(total_decay[..., None, None] * carried + update, "seq", 1)

    state_in = lax.fori_loop(0, lax.axis_size("seq") - 1, relay_step, jnp.zeros_like(update))
    growth = jnp.exp(cumulative)
    readout = jnp.einsum("btn,bhpn->bthp", out_keys_f, state_in, precision=PRECISE)
    carried_part = growth[..., None] * readout
    mixed_out = local_part + carried_part + skip_gain[:, None] * values_f
    mixed_flat = mixed_out.reshape(1, block_len, INNER)
    normed_out_f, gate_back = jax.vjp(gated_norm, mixed_flat, gate_in, gate_full.astype(WIDE_TYPE))
    normed_out = normed_out_f.astype(NARROW_TYPE)
    branch = jnp.einsum("bck,kd->bcd", normed_out, out_full, preferred_element_type=WIDE_TYPE)
    outputs = (inputs_f + valid_mask[..., None] * branch).astype(NARROW_TYPE)
    kept = {
        "norm_back": norm_back,
        "gate_back": gate_back,
        "normed": normed,
        "extended": extended,
        "conv_out": conv_out,
        "values": values,
        "values_f": values_f,
        "in_keys": in_keys,
        "out_keys": out_keys,
        "in_keys_f": in_keys_f,
        "out_keys_f": out_keys_f,
        "valid_mask": valid_mask,
        "step_pre": step_pre,
        "step_size": step_size,
        "log_decay": log_decay,
        "cumulative": cumulative,
        "affinity": affinity,
        "tail_decay": tail_decay,
        "weights_in": weights_in,
        "weighted": weighted,
        "total_decay": total_decay,
        "state_in": state_in,
        "growth": growth,
        "carried_part": carried_part,
        "normed_out": normed_out,
    }
    return (outputs, kept)


def backward_micro(cot, kept, in_back, out_back, small):
    conv_weight, conv_bias, decay_log, step_bias, skip_gain = small
    block_len = cot.shape[1]
    values = kept["values"]
    values_f = kept["values_f"]
    in_keys = kept["in_keys"]
    out_keys = kept["out_keys"]
    in_keys_f = kept["in_keys_f"]
    out_keys_f = kept["out_keys_f"]
    valid_mask = kept["valid_mask"]
    step_size = kept["step_size"]
    cumulative = kept["cumulative"]
    affinity = kept["affinity"]
    state_in = kept["state_in"]
    growth = kept["growth"]
    total_decay = kept["total_decay"]
    weights_in = kept["weights_in"]
    tail_decay = kept["tail_decay"]
    extended = kept["extended"]
    conv_out = kept["conv_out"]
    decay_rates = jnp.exp(decay_log)
    segment = segment_of(cumulative, block_len)
    mixing = (affinity[..., None] * segment * step_size[:, None, :, :]).astype(NARROW_TYPE)
    cot_f = cot.astype(WIDE_TYPE)
    masked_cot = (cot_f * valid_mask[..., None]).astype(NARROW_TYPE)
    grad_out_w = jnp.einsum(
        "bck,bcd->kd", kept["normed_out"], masked_cot, preferred_element_type=WIDE_TYPE
    )
    grad_normed_out = jnp.einsum(
        "bcd,kd->bck", masked_cot, out_back, preferred_element_type=WIDE_TYPE
    )
    grad_mixed, grad_gate_in, grad_gate_gain = kept["gate_back"](grad_normed_out)
    grad_mixed = grad_mixed.reshape(1, block_len, HEADS, HDIM)
    grad_skip = jnp.sum(grad_mixed * values_f, axis=(0, 1, 3))
    grad_core = grad_mixed.astype(NARROW_TYPE)
    grad_core_f = grad_core.astype(WIDE_TYPE)
    grad_values = skip_gain[:, None] * grad_mixed
    grad_mixing = jnp.einsum("bthp,bshp->btsh", grad_core, values, preferred_element_type=WIDE_TYPE)
    grad_values = grad_values + jnp.einsum(
        "btsh,bthp->bshp", mixing, grad_core, preferred_element_type=WIDE_TYPE
    )
    through = grad_mixing * segment * affinity[..., None]
    grad_step = jnp.sum(through, axis=1)
    edge_terms = through * step_size[:, None, :, :]
    grad_cumul = jnp.sum(edge_terms, axis=2) - jnp.sum(edge_terms, axis=1)
    grad_affinity = jnp.sum(grad_mixing * segment * step_size[:, None, :, :], axis=3).astype(
        NARROW_TYPE
    )
    grad_out_keys = jnp.einsum(
        "bts,bsn->btn", grad_affinity, in_keys, preferred_element_type=WIDE_TYPE
    )
    grad_in_keys = jnp.einsum(
        "bts,btn->bsn", grad_affinity, out_keys, preferred_element_type=WIDE_TYPE
    )
    scaled_grad = growth[..., None] * grad_core_f
    grad_out_keys = grad_out_keys + jnp.einsum(
        "bthp,bhpn->btn", scaled_grad, state_in, precision=PRECISE
    )
    grad_cumul = grad_cumul + jnp.sum(grad_core_f * kept["carried_part"], axis=3)
    local_state_grad = jnp.einsum("bthp,btn->bhpn", scaled_grad, out_keys_f, precision=PRECISE)

    def relay_back(iteration, carried):
        return from_behind(total_decay[..., None, None] * carried + local_state_grad, "seq", -1)

    grad_state_out = lax.fori_loop(
        0, lax.axis_size("seq") - 1, relay_back, jnp.zeros_like(local_state_grad)
    )
    grad_total = jnp.sum(grad_state_out * state_in, axis=(2, 3))
    grad_weighted = jnp.einsum("bhpn,btn->bthp", grad_state_out, in_keys_f, precision=PRECISE)
    grad_in_keys = grad_in_keys + jnp.einsum(
        "bthp,bhpn->btn", kept["weighted"], grad_state_out, precision=PRECISE
    )
    grad_values = grad_values + weights_in[..., None] * grad_weighted
    grad_weights_in = jnp.sum(grad_weighted * values_f, axis=3)
    grad_step = grad_step + grad_weights_in * tail_decay
    weight_terms = grad_weights_in * weights_in
    grad_cumul = grad_cumul - weight_terms
    grad_cumul = grad_cumul.at[:, -1].add(jnp.sum(weight_terms, axis=1) + grad_total * total_decay)
    grad_log_decay = jnp.flip(jnp.cumsum(jnp.flip(grad_cumul, 1), axis=1), 1)
    grad_step = grad_step - decay_rates * grad_log_decay
    grad_decay_log = jnp.sum(grad_log_decay * kept["log_decay"], axis=(0, 1))
    grad_step_raw = grad_step * valid_mask[..., None] * jax.nn.sigmoid(kept["step_pre"])
    grad_step_bias = jnp.sum(grad_step_raw, axis=(0, 1))
    grad_activated = jnp.concatenate(
        [grad_values.reshape(1, block_len, INNER), grad_in_keys, grad_out_keys], axis=-1
    )
    sigmoid_conv = jax.nn.sigmoid(conv_out)
    grad_conv = grad_activated * sigmoid_conv * (1.0 + conv_out * (1.0 - sigmoid_conv))
    grad_conv_bias = jnp.sum(grad_conv, axis=(0, 1))
    grad_conv_weight = jnp.stack(
        [
            jnp.sum(grad_conv * extended[:, offset : offset + block_len], axis=(0, 1))
            for offset in range(KCONV)
        ]
    )
    grad_extended = jnp.zeros_like(extended)
    for offset in range(KCONV):
        grad_extended = grad_extended.at[:, offset : offset + block_len].add(
            conv_weight[offset] * grad_conv
        )
    returned = from_behind(grad_extended[:, : KCONV - 1], "seq", -1)
    grad_conv_in = grad_extended[:, KCONV - 1 :].at[:, block_len - (KCONV - 1) :].add(returned)
    grad_projected = jnp.concatenate([grad_gate_in, grad_conv_in, grad_step_raw], axis=-1).astype(
        NARROW_TYPE
    )
    grad_in_w = jnp.einsum(
        "bcd,bck->dk", kept["normed"], grad_projected, preferred_element_type=WIDE_TYPE
    )
    grad_normed = jnp.einsum(
        "bck,dk->bcd", grad_projected, in_back, preferred_element_type=WIDE_TYPE
    )
    grad_inputs, grad_norm_gain = kept["norm_back"](grad_normed)
    grad_tokens = (cot_f + grad_inputs).astype(NARROW_TYPE)
    sums = (
        grad_in_w,
        grad_out_w,
        grad_norm_gain,
        grad_gate_gain,
        grad_conv_weight,
        grad_conv_bias,
        grad_decay_log,
        grad_step_bias,
        grad_skip,
    )
    return (grad_tokens, sums)


def per_device(
    tokens,
    lengths,
    dealing,
    cotangent,
    in_weight,
    out_weight,
    norm_gain,
    gate_gain,
    conv_weight,
    conv_bias,
    decay_log,
    step_bias,
    skip_gain,
):
    full = (
        lax.all_gather(in_weight, ("dp", "seq"), axis=0, tiled=True),
        lax.all_gather(out_weight, ("dp", "seq"), axis=0, tiled=True),
        lax.all_gather(norm_gain, ("dp", "seq"), axis=0, tiled=True),
        lax.all_gather(gate_gain, ("dp", "seq"), axis=0, tiled=True),
    )
    small = (conv_weight, conv_bias, decay_log, step_bias, skip_gain)
    dealt_tokens, dealt_lengths, anchor = deal_sequences(tokens, lengths, dealing)
    micro_count = tokens.shape[0]
    output_list = []
    kept_list = []
    for micro in range(micro_count):
        result, kept = forward_micro(
            dealt_tokens[micro], dealt_lengths[micro : micro + 1], full, small
        )
        output_list.append(result)
        kept_list.append(kept)
    in_back, out_back = (
        lax.all_gather(in_weight, ("dp", "seq"), axis=0, tiled=True),
        lax.all_gather(out_weight, ("dp", "seq"), axis=0, tiled=True),
    )
    grad_list = []
    totals = None
    for micro in range(micro_count):
        grad_tok, sums = backward_micro(
            cotangent[micro], kept_list[micro], in_back, out_back, small
        )
        grad_list.append(grad_tok)
        totals = sums if totals is None else jax.tree.map(jnp.add, totals, sums)
    outputs = jnp.stack(output_list, axis=0)
    grad_dealt = jnp.stack(grad_list, axis=0)
    grad_tokens = return_sequences(grad_dealt, anchor)
    owned = (
        lax.psum_scatter(totals[0], ("dp", "seq"), scatter_dimension=0, tiled=True),
        lax.psum_scatter(totals[1], ("dp", "seq"), scatter_dimension=0, tiled=True),
        lax.psum_scatter(totals[2], ("dp", "seq"), scatter_dimension=0, tiled=True),
        lax.psum_scatter(totals[3], ("dp", "seq"), scatter_dimension=0, tiled=True),
    )
    small_sums = lax.psum((totals[4], totals[5], totals[6], totals[7], totals[8]), ("dp", "seq"))
    return (
        outputs,
        grad_tokens,
        owned[0],
        owned[1],
        owned[2],
        owned[3],
        small_sums[0],
        small_sums[1],
        small_sums[2],
        small_sums[3],
        small_sums[4],
    )


def solution(mesh):
    in_specs = (
        P(None, "dp", "seq", None),
        P(None, "dp"),
        P(None, "dp"),
        P(None, "dp", "seq", None),
        P(("dp", "seq"), None),
        P(("dp", "seq"), None),
        P(("dp", "seq")),
        P(("dp", "seq")),
        P(),
        P(),
        P(),
        P(),
        P(),
    )
    out_specs = (
        P(None, "dp", "seq", None),
        P(None, "dp", "seq", None),
        P(("dp", "seq"), None),
        P(("dp", "seq"), None),
        P(("dp", "seq")),
        P(("dp", "seq")),
        P(),
        P(),
        P(),
        P(),
        P(),
    )
    return jax.shard_map(
        per_device, mesh=mesh, in_specs=in_specs, out_specs=out_specs, check_vma=False
    )
```

profile of v0, /device:TPU:0, one launch (start us, length us, event | category | flops | bytes accessed | tf_op | source)
XLA Modules:
  0.0 838.7 jit_solution(9764396478869981898)
XLA Ops:
  18.4 16.4 %collective-permute-done.25 = s32[2]{0:T(128)S(1)} collective-permute-done((s32[2]{0:T(128)S(1)}, s32[2]{0:T(128)S(1)}, u32[]{:S(2)}, u32[]{:S(2)}) %collective-permute-start.25) | collective-permute-done | bytes 40 | tf_op jit(solution)/shard_map/ppermute | solution.py:30
  35.6 41.3 %all-reduce.8 = (bf16[768]{0:T(1024)(128)(2,1)S(1)}, bf16[1536]{0:T(1024)(128)(2,1)S(1)}) all-reduce(bf16[768]{0:T(1024)(128)(2,1)S(1)} %dynamic-update-slice.42, bf16[1536]{0:T(1024)(128)(2,1)S(1)} %dynamic-update-slice.43), channel_id=1, replica_groups=mesh['dp'=8,'seq'=4] {'dp','seq'}, use_global_device_ids=true, to_apply=%add.2 | all-reduce | flops 2304 | bytes 9216
  88.7 15.4 %collective-permute-done.7 = s32[2]{0:T(128)S(1)} collective-permute-done((s32[2]{0:T(128)S(1)}, s32[2]{0:T(128)S(1)}, u32[]{:S(2)}, u32[]{:S(2)}) %collective-permute-start.7) | collective-permute-done | bytes 40 | tf_op jit(solution)/shard_map/ppermute | solution.py:30
  113.1 15.5 %collective-permute-done.8 = s32[2]{0:T(128)S(1)} collective-permute-done((s32[2]{0:T(128)S(1)}, s32[2]{0:T(128)S(1)}, u32[]{:S(2)}, u32[]{:S(2)}) %collective-permute-start.8) | collective-permute-done | bytes 40 | tf_op jit(solution)/shard_map/ppermute | solution.py:30
  203.9 58.4 %while.52 = (s32[]{:T(128)}, f32[1,24,64,128]{3,2,1,0:T(8,128)S(1)}, f32[1,24]{1,0:T(1,128)S(1)}, f32[1,24,64,128]{3,2,1,0:T(8,128)S(1)}, s32[]{:T(128)}) while((s32[]{:T(128)}, f32[1,24,64,128]{3,2,1,0:T(8,128)S(1)}, f32[1,24]{1,0:T(1,128)S(1)}, f32[1,24,64,128]{3,2,1,0:T(8,128)S(1)}, s32[]{:T(128)}) %tuple.224), condition=%wide.region_4.5_spmd, body=%wide.region_3.4_spmd.sunk | while | flops 393218 | bytes 5505221 | solution.py:153
  205.7 16.6 %collective-permute-done = f32[1,24,64,128]{3,2,1,0:T(8,128)S(1)} collective-permute-done((f32[1,24,64,128]{3,2,1,0:T(8,128)S(1)}, f32[1,24,64,128]{3,2,1,0:T(8,128)S(1)}, u32[]{:S(2)}, u32[]{:S(2)}) %collective-permute-start) | collective-permute-done | bytes 786464 | tf_op jit(solution)/shard_map/while/body/eval_jaxpr/ppermute | solution.py:36
  226.9 15.8 %collective-permute-done = f32[1,24,64,128]{3,2,1,0:T(8,128)S(1)} collective-permute-done((f32[1,24,64,128]{3,2,1,0:T(8,128)S(1)}, f32[1,24,64,128]{3,2,1,0:T(8,128)S(1)}, u32[]{:S(2)}, u32[]{:S(2)}) %collective-permute-start) | collective-permute-done | bytes 786464 | tf_op jit(solution)/shard_map/while/body/eval_jaxpr/ppermute | solution.py:36
  247.3 14.9 %collective-permute-done = f32[1,24,64,128]{3,2,1,0:T(8,128)S(1)} collective-permute-done((f32[1,24,64,128]{3,2,1,0:T(8,128)S(1)}, f32[1,24,64,128]{3,2,1,0:T(8,128)S(1)}, u32[]{:S(2)}, u32[]{:S(2)}) %collective-permute-start) | collective-permute-done | bytes 786464 | tf_op jit(solution)/shard_map/while/body/eval_jaxpr/ppermute | solution.py:36
  270.7 60.6 %while.53 = (s32[]{:T(128)}, f32[1,24,64,128]{3,2,1,0:T(8,128)S(1)}, f32[1,24]{1,0:T(1,128)S(1)}, f32[1,24,64,128]{3,2,1,0:T(8,128)}, s32[]{:T(128)}) while((s32[]{:T(128)}, f32[1,24,64,128]{3,2,1,0:T(8,128)S(1)}, f32[1,24]{1,0:T(1,128)S(1)}, f32[1,24,64,128]{3,2,1,0:T(8,128)}, s32[]{:T(128)}) %tuple.222), condition=%wide.region_10.11_spmd, body=%wide.region_9.10_spmd.sunk | while | flops 393218 | bytes 5505221 | solution.py:153
  277.3 14.4 %collective-permute-done.1 = f32[1,24,64,128]{3,2,1,0:T(8,128)S(1)} collective-permute-done((f32[1,24,64,128]{3,2,1,0:T(8,128)}, f32[1,24,64,128]{3,2,1,0:T(8,128)S(1)}, u32[]{:S(2)}, u32[]{:S(2)}) %collective-permute-start.1) | collective-permute-done | bytes 786464 | tf_op jit(solution)/shard_map/while/body/eval_jaxpr/ppermute | solution.py:36
  298.2 13.5 %collective-permute-done.1 = f32[1,24,64,128]{3,2,1,0:T(8,128)S(1)} collective-permute-done((f32[1,24,64,128]{3,2,1,0:T(8,128)}, f32[1,24,64,128]{3,2,1,0:T(8,128)S(1)}, u32[]{:S(2)}, u32[]{:S(2)}) %collective-permute-start.1) | collective-permute-done | bytes 786464 | tf_op jit(solution)/shard_map/while/body/eval_jaxpr/ppermute | solution.py:36
  318.2 12.7 %collective-permute-done.1 = f32[1,24,64,128]{3,2,1,0:T(8,128)S(1)} collective-permute-done((f32[1,24,64,128]{3,2,1,0:T(8,128)}, f32[1,24,64,128]{3,2,1,0:T(8,128)S(1)}, u32[]{:S(2)}, u32[]{:S(2)}) %collective-permute-start.1) | collective-permute-done | bytes 786464 | tf_op jit(solution)/shard_map/while/body/eval_jaxpr/ppermute | solution.py:36
  351.0 51.5 %while.54 = (s32[]{:T(128)}, f32[1,24,64,128]{3,2,1,0:T(8,128)S(1)}, f32[1,24]{1,0:T(1,128)S(1)}, f32[1,24,64,128]{3,2,1,0:T(8,128)S(1)}, s32[]{:T(128)}) while((s32[]{:T(128)}, f32[1,24,64,128]{3,2,1,0:T(8,128)S(1)}, f32[1,24]{1,0:T(1,128)S(1)}, f32[1,24,64,128]{3,2,1,0:T(8,128)S(1)}, s32[]{:T(128)}) %tuple.225), condition=%wide.region_14.15_spmd, body=%wide.region_13.14_spmd.sunk | while | flops 393218 | bytes 5505221 | solution.py:257
  353.4 15.5 %collective-permute-done.2 = f32[1,24,64,128]{3,2,1,0:T(8,128)S(1)} collective-permute-done((f32[1,24,64,128]{3,2,1,0:T(8,128)}, f32[1,24,64,128]{3,2,1,0:T(8,128)S(1)}, u32[]{:S(2)}, u32[]{:S(2)}) %collective-permute-start.2) | collective-permute-done | bytes 786464 | tf_op jit(solution)/shard_map/while/body/eval_jaxpr/ppermute | solution.py:36
  371.2 15.3 %collective-permute-done.2 = f32[1,24,64,128]{3,2,1,0:T(8,128)S(1)} collective-permute-done((f32[1,24,64,128]{3,2,1,0:T(8,128)}, f32[1,24,64,128]{3,2,1,0:T(8,128)S(1)}, u32[]{:S(2)}, u32[]{:S(2)}) %collective-permute-start.2) | collective-permute-done | bytes 786464 | tf_op jit(solution)/shard_map/while/body/eval_jaxpr/ppermute | solution.py:36
  388.9 13.7 %collective-permute-done.2 = f32[1,24,64,128]{3,2,1,0:T(8,128)S(1)} collective-permute-done((f32[1,24,64,128]{3,2,1,0:T(8,128)}, f32[1,24,64,128]{3,2,1,0:T(8,128)S(1)}, u32[]{:S(2)}, u32[]{:S(2)}) %collective-permute-start.2) | collective-permute-done | bytes 786464 | tf_op jit(solution)/shard_map/while/body/eval_jaxpr/ppermute | solution.py:36
  421.4 51.6 %while.55 = (s32[]{:T(128)}, f32[1,24,64,128]{3,2,1,0:T(8,128)S(1)}, f32[1,24]{1,0:T(1,128)S(1)}, f32[1,24,64,128]{3,2,1,0:T(8,128)S(1)}, s32[]{:T(128)}) while((s32[]{:T(128)}, f32[1,24,64,128]{3,2,1,0:T(8,128)S(1)}, f32[1,24]{1,0:T(1,128)S(1)}, f32[1,24,64,128]{3,2,1,0:T(8,128)S(1)}, s32[]{:T(128)}) %tuple.223), condition=%wide.region_28.29_spmd, body=%wide.region_27.28_spmd.sunk | while | flops 393218 | bytes 5505221 | solution.py:257
  422.8 16.3 %collective-permute-done.3 = f32[1,24,64,128]{3,2,1,0:T(8,128)S(1)} collective-permute-done((f32[1,24,64,128]{3,2,1,0:T(8,128)S(1)}, f32[1,24,64,128]{3,2,1,0:T(8,128)S(1)}, u32[]{:S(2)}, u32[]{:S(2)}) %collective-permute-start.3) | collective-permute-done | bytes 786464 | tf_op jit(solution)/shard_map/while/body/eval_jaxpr/ppermute | solution.py:36
  440.5 18.1 %collective-permute-done.3 = f32[1,24,64,128]{3,2,1,0:T(8,128)S(1)} collective-permute-done((f32[1,24,64,128]{3,2,1,0:T(8,128)S(1)}, f32[1,24,64,128]{3,2,1,0:T(8,128)S(1)}, u32[]{:S(2)}, u32[]{:S(2)}) %collective-permute-start.3) | collective-permute-done | bytes 786464 | tf_op jit(solution)/shard_map/while/body/eval_jaxpr/ppermute | solution.py:36
  460.1 12.9 %collective-permute-done.3 = f32[1,24,64,128]{3,2,1,0:T(8,128)S(1)} collective-permute-done((f32[1,24,64,128]{3,2,1,0:T(8,128)S(1)}, f32[1,24,64,128]{3,2,1,0:T(8,128)S(1)}, u32[]{:S(2)}, u32[]{:S(2)}) %collective-permute-start.3) | collective-permute-done | bytes 786464 | tf_op jit(solution)/shard_map/while/body/eval_jaxpr/ppermute | solution.py:36
  684.4 17.6 %collective-permute-done.31 = s32[2]{0:T(128)S(1)} collective-permute-done((s32[2]{0:T(128)S(1)}, s32[2]{0:T(128)S(1)}, u32[]{:S(2)}, u32[]{:S(2)}) %collective-permute-start.31) | collective-permute-done | bytes 40 | tf_op jit(solution)/shard_map/ppermute | solution.py:30
  708.5 18.1 %collective-permute-done.33 = s32[2]{0:T(128)S(1)} collective-permute-done((s32[2]{0:T(128)S(1)}, s32[2]{0:T(128)S(1)}, u32[]{:S(2)}, u32[]{:S(2)}) %collective-permute-start.33) | collective-permute-done | bytes 40 | tf_op jit(solution)/shard_map/ppermute | solution.py:30
  730.9 26.1 %collective-permute-done.34 = s32[2]{0:T(128)S(1)} collective-permute-done((s32[2]{0:T(128)S(1)}, s32[2]{0:T(128)S(1)}, u32[]{:S(2)}, u32[]{:S(2)}) %collective-permute-start.34) | collective-permute-done | bytes 40 | tf_op jit(solution)/shard_map/ppermute | solution.py:30
  786.0 42.4 %all-reduce.7 = (f32[768]{0:T(1024)S(1)}, f32[1536]{0:T(1024)S(1)}, f32[4,1792]{1,0:T(4,128)}, f32[1792]{0:T(1024)}, f32[24]{0:T(128)}, /*index=5*/f32[24]{0:T(128)}, f32[24]{0:T(128)}) all-reduce(f32[768]{0:T(1024)S(1)} %add.522, f32[1536]{0:T(1024)} %add.523, ...), channel_id=4, replica_groups=mesh['dp'=8,'seq'=4] {'dp','seq'}, use_global_device_ids=true, to_apply=%region_44.45.clone | all-reduce | flops 11336 | bytes 90688
  (629 shorter events, 449.6 us)
Async XLA Ops:
  7.2 125.6 %all-gather.5.cloned.1.call-start = ((), (), s32[]{:S(2)}) async-start(), calls=%async_computation.3 | async-start | bytes 2433024 | tf_op jit(solution)/shard_map/all_gather | solution.py:337
  7.9 134.3 %all-gather.3.cloned.1.call-start = ((), (), s32[]{:S(2)}) async-start(), calls=%async_computation.2 | async-start | bytes 5474304 | tf_op jit(solution)/shard_map/all_gather | solution.py:336
  8.7 823.3 %reduce-scatter.5.cloned.1.call-start = ((), (), s32[]{:S(2)}) async-start(), calls=%async_computation.4 | async-start | bytes 4866048 | tf_op jit(solution)/shard_map/reduce_scatter | solution.py:369
  13.4 21.4 %collective-permute-start.11 = (bf16[2,1,256,768]{3,2,1,0:T(8,128)(2,1)S(1)}, bf16[2,1,256,768]{3,2,1,0:T(8,128)(2,1)S(1)}, u32[]{:S(2)}, u32[]{:S(2)}) collective-permute-start(bf16[2,1,256,768]{3,2,1,0:T(8,128)(2,1)S(1)} %broadcast_select_fusion.6), channel_id=1, source_target_pairs={{0,8},{4,12},{8,0},{12,4},{16,24},{20,28},{24,16},{28,20},{1,9},{5... | collective-permute-start | bytes 2359304 | tf_op jit(solution)/shard_map/ppermute | solution.py:30
  16.3 18.5 %collective-permute-start.25 = (s32[2]{0:T(128)S(1)}, s32[2]{0:T(128)S(1)}, u32[]{:S(2)}, u32[]{:S(2)}) collective-permute-start(s32[2]{0:T(128)S(1)} %get-tuple-element.354), channel_id=1, source_target_pairs={{0,8},{4,12},{8,0},{12,4},{16,24},{20,28},{24,16},{28,20},{1,9},{5... | collective-permute-start | bytes 32 | tf_op jit(solution)/shard_map/ppermute | solution.py:30
  35.0 47.1 %collective-permute-start.12 = (bf16[2,1,256,768]{3,2,1,0:T(8,128)(2,1)S(1)}, bf16[2,1,256,768]{3,2,1,0:T(8,128)(2,1)S(1)}, u32[]{:S(2)}, u32[]{:S(2)}) collective-permute-start(bf16[2,1,256,768]{3,2,1,0:T(8,128)(2,1)S(1)} %broadcast_select_fusion.7), channel_id=1, source_target_pairs={{0,4},{4,0},{8,12},{12,8},{16,20},{20,16},{24,28},{28,24},{1,5},{5... | collective-permute-start | bytes 2359304 | tf_op jit(solution)/shard_map/ppermute | solution.py:30
  82.2 22.0 %collective-permute-start.13 = (bf16[2,1,256,768]{3,2,1,0:T(8,128)(2,1)S(1)}, bf16[2,1,256,768]{3,2,1,0:T(8,128)(2,1)S(1)}, u32[]{:S(2)}, u32[]{:S(2)}) collective-permute-start(bf16[2,1,256,768]{3,2,1,0:T(8,128)(2,1)S(1)} %broadcast_select_fusion.8), channel_id=1, source_target_pairs={{0,16},{4,20},{8,24},{12,28},{16,0},{20,4},{24,8},{28,12},{1,17},{... | collective-permute-start | bytes 2359304 | tf_op jit(solution)/shard_map/ppermute | solution.py:30
  104.3 25.0 %collective-permute-start.14 = (bf16[2,1,256,768]{3,2,1,0:T(8,128)(2,1)S(1)}, bf16[2,1,256,768]{3,2,1,0:T(8,128)(2,1)S(1)}, u32[]{:S(2)}, u32[]{:S(2)}) collective-permute-start(bf16[2,1,256,768]{3,2,1,0:T(8,128)(2,1)S(1)} %broadcast_select_fusion.9), channel_id=1, source_target_pairs={{0,8},{4,12},{8,0},{12,4},{16,24},{20,28},{24,16},{28,20},{1,9},{5... | collective-permute-start | bytes 2359304 | tf_op jit(solution)/shard_map/ppermute | solution.py:30
  110.9 17.7 %collective-permute-start.20 = (s32[2]{0:T(128)S(1)}, s32[2]{0:T(128)S(1)}, u32[]{:S(2)}, u32[]{:S(2)}) collective-permute-start(s32[2]{0:T(128)S(1)} %get-tuple-element.415), channel_id=1, source_target_pairs={{0,8},{4,12},{8,0},{12,4},{16,24},{20,28},{24,16},{28,20},{1,9},{5... | collective-permute-start | bytes 32 | tf_op jit(solution)/shard_map/ppermute | solution.py:30
  159.9 20.2 %collective-permute-start.23 = (f32[1,3,1792]{2,0,1:T(1,128)}, f32[1,3,1792]{2,0,1:T(1,128)}, u32[]{:S(2)}, u32[]{:S(2)}) collective-permute-start(f32[1,3,1792]{2,0,1:T(1,128)} %copy.123), channel_id=1, source_target_pairs={{0,1},{1,2},{2,3},{4,5},{5,6},{6,7},{8,9},{9,10},{10,11},{12,13},{... | collective-permute-start | bytes 64520 | tf_op jit(solution)/shard_map/ppermute | solution.py:36
  204.0 18.3 %collective-permute-start = (f32[1,24,64,128]{3,2,1,0:T(8,128)S(1)}, f32[1,24,64,128]{3,2,1,0:T(8,128)S(1)}, u32[]{:S(2)}, u32[]{:S(2)}) collective-permute-start(f32[1,24,64,128]{3,2,1,0:T(8,128)S(1)} %multiply_add_fusion.18), channel_id=1, source_target_pairs={{0,1},{1,2},{2,3},{4,5},{5,6},{6,7},{8,9},{9,10},{10,11},{12,13},{... | collective-permute-start | bytes 2359304 | tf_op jit(solution)/shard_map/while/body/eval_jaxpr/ppermute | solution.py:36
  222.5 20.2 %collective-permute-start = (f32[1,24,64,128]{3,2,1,0:T(8,128)S(1)}, f32[1,24,64,128]{3,2,1,0:T(8,128)S(1)}, u32[]{:S(2)}, u32[]{:S(2)}) collective-permute-start(f32[1,24,64,128]{3,2,1,0:T(8,128)S(1)} %multiply_add_fusion.18), channel_id=1, source_target_pairs={{0,1},{1,2},{2,3},{4,5},{5,6},{6,7},{8,9},{9,10},{10,11},{12,13},{... | collective-permute-start | bytes 2359304 | tf_op jit(solution)/shard_map/while/body/eval_jaxpr/ppermute | solution.py:36
  242.9 19.4 %collective-permute-start = (f32[1,24,64,128]{3,2,1,0:T(8,128)S(1)}, f32[1,24,64,128]{3,2,1,0:T(8,128)S(1)}, u32[]{:S(2)}, u32[]{:S(2)}) collective-permute-start(f32[1,24,64,128]{3,2,1,0:T(8,128)S(1)} %multiply_add_fusion.18), channel_id=1, source_target_pairs={{0,1},{1,2},{2,3},{4,5},{5,6},{6,7},{8,9},{9,10},{10,11},{12,13},{... | collective-permute-start | bytes 2359304 | tf_op jit(solution)/shard_map/while/body/eval_jaxpr/ppermute | solution.py:36
  272.9 18.8 %collective-permute-start.1 = (f32[1,24,64,128]{3,2,1,0:T(8,128)}, f32[1,24,64,128]{3,2,1,0:T(8,128)S(1)}, u32[]{:S(2)}, u32[]{:S(2)}) collective-permute-start(f32[1,24,64,128]{3,2,1,0:T(8,128)} %multiply_add_fusion.19), channel_id=1, source_target_pairs={{0,1},{1,2},{2,3},{4,5},{5,6},{6,7},{8,9},{9,10},{10,11},{12,13},{... | collective-permute-start | bytes 2359304 | tf_op jit(solution)/shard_map/while/body/eval_jaxpr/ppermute | solution.py:36
  293.9 17.9 %collective-permute-start.1 = (f32[1,24,64,128]{3,2,1,0:T(8,128)}, f32[1,24,64,128]{3,2,1,0:T(8,128)S(1)}, u32[]{:S(2)}, u32[]{:S(2)}) collective-permute-start(f32[1,24,64,128]{3,2,1,0:T(8,128)} %multiply_add_fusion.19), channel_id=1, source_target_pairs={{0,1},{1,2},{2,3},{4,5},{5,6},{6,7},{8,9},{9,10},{10,11},{12,13},{... | collective-permute-start | bytes 2359304 | tf_op jit(solution)/shard_map/while/body/eval_jaxpr/ppermute | solution.py:36
  439.2 19.4 %collective-permute-start.3 = (f32[1,24,64,128]{3,2,1,0:T(8,128)S(1)}, f32[1,24,64,128]{3,2,1,0:T(8,128)S(1)}, u32[]{:S(2)}, u32[]{:S(2)}) collective-permute-start(f32[1,24,64,128]{3,2,1,0:T(8,128)S(1)} %multiply_add_fusion.21), channel_id=1, source_target_pairs={{1,0},{2,1},{3,2},{5,4},{6,5},{7,6},{9,8},{10,9},{11,10},{13,12},{... | collective-permute-start | bytes 2359304 | tf_op jit(solution)/shard_map/while/body/eval_jaxpr/ppermute | solution.py:36
  547.1 284.9 %reduce-scatter.7.cloned.1.call-start = ((), (), s32[]{:S(2)}) async-start(), calls=%async_computation.5 | async-start | bytes 10948608
  682.3 19.8 %collective-permute-start.39 = (bf16[2,1,256,768]{3,2,1,0:T(8,128)(2,1)S(1)}, bf16[2,1,256,768]{3,2,1,0:T(8,128)(2,1)S(1)}, u32[]{:S(2)}, u32[]{:S(2)}) collective-permute-start(bf16[2,1,256,768]{3,2,1,0:T(8,128)(2,1)S(1)} %broadcast_select_fusion), channel_id=1, source_target_pairs={{0,8},{4,12},{8,0},{12,4},{16,24},{20,28},{24,16},{28,20},{1,9},{5... | collective-permute-start | bytes 2359304 | tf_op jit(solution)/shard_map/ppermute | solution.py:30
  683.5 18.5 %collective-permute-start.31 = (s32[2]{0:T(128)S(1)}, s32[2]{0:T(128)S(1)}, u32[]{:S(2)}, u32[]{:S(2)}) collective-permute-start(s32[2]{0:T(128)S(1)} %fusion.180), channel_id=1, source_target_pairs={{0,8},{4,12},{8,0},{12,4},{16,24},{20,28},{24,16},{28,20},{1,9},{5... | collective-permute-start | bytes 32 | tf_op jit(solution)/shard_map/ppermute | solution.py:30
  705.9 20.7 %collective-permute-start.41 = (bf16[2,1,256,768]{3,2,1,0:T(8,128)(2,1)}, bf16[2,1,256,768]{3,2,1,0:T(8,128)(2,1)}, u32[]{:S(2)}, u32[]{:S(2)}) collective-permute-start(bf16[2,1,256,768]{3,2,1,0:T(8,128)(2,1)} %broadcast_select_fusion.2), channel_id=1, source_target_pairs={{0,16},{4,20},{8,24},{12,28},{16,0},{20,4},{24,8},{28,12},{1,17},{... | collective-permute-start | bytes 2359304 | tf_op jit(solution)/shard_map/ppermute | solution.py:30
  708.4 18.2 %collective-permute-start.33 = (s32[2]{0:T(128)S(1)}, s32[2]{0:T(128)S(1)}, u32[]{:S(2)}, u32[]{:S(2)}) collective-permute-start(s32[2]{0:T(128)S(1)} %fusion.182), channel_id=1, source_target_pairs={{0,16},{4,20},{8,24},{12,28},{16,0},{20,4},{24,8},{28,12},{1,17},{... | collective-permute-start | bytes 32 | tf_op jit(solution)/shard_map/ppermute | solution.py:30
  728.8 30.0 %collective-permute-start.42 = (bf16[2,1,256,768]{3,2,1,0:T(8,128)(2,1)S(1)}, bf16[2,1,256,768]{3,2,1,0:T(8,128)(2,1)S(1)}, u32[]{:S(2)}, u32[]{:S(2)}) collective-permute-start(bf16[2,1,256,768]{3,2,1,0:T(8,128)(2,1)S(1)} %broadcast_select_fusion.3), channel_id=1, source_target_pairs={{0,8},{4,12},{8,0},{12,4},{16,24},{20,28},{24,16},{28,20},{1,9},{5... | collective-permute-start | bytes 2359304 | tf_op jit(solution)/shard_map/ppermute | solution.py:30
  728.9 28.1 %collective-permute-start.34 = (s32[2]{0:T(128)S(1)}, s32[2]{0:T(128)S(1)}, u32[]{:S(2)}, u32[]{:S(2)}) collective-permute-start(s32[2]{0:T(128)S(1)} %fusion.183), channel_id=1, source_target_pairs={{0,8},{4,12},{8,0},{12,4},{16,24},{20,28},{24,16},{28,20},{1,9},{5... | collective-permute-start | bytes 32 | tf_op jit(solution)/shard_map/ppermute | solution.py:30
  759.7 69.8 %collective-permute-start.43 = (bf16[2,1,256,768]{3,2,1,0:T(8,128)(2,1)}, bf16[2,1,256,768]{3,2,1,0:T(8,128)(2,1)}, u32[]{:S(2)}, u32[]{:S(2)}) collective-permute-start(bf16[2,1,256,768]{3,2,1,0:T(8,128)(2,1)} %broadcast_select_fusion.4), channel_id=1, source_target_pairs={{0,4},{4,0},{8,12},{12,8},{16,20},{20,16},{24,28},{28,24},{1,5},{5... | collective-permute-start | bytes 2359304 | tf_op jit(solution)/shard_map/ppermute | solution.py:30
  (179 other events, 1488.7 us)
Sparse Core Ops, SparseCore 0:
  10.8 60.2 all-gather.4
  73.9 68.2 all-gather.2
  547.2 108.7 reduce-scatter.4
  670.8 147.9 reduce-scatter.6
where the time goes:
time: 852 us; the launch traced here: 839 us
  waiting for transfers between devices  309 us (36%)
  local copies, waits for them, and re-layouts  145 us (17%)
  other arithmetic  120 us (14%)
  matrix products  96.7 us (11%)
  blocking collectives  83.7 us (10%)
  starting transfers between devices  67.8 us (8%)
  between operations  15.9 us (2%)
    ppermute x16, waiting for transfers between devices, from_behind(): return lax.ppermute(block, axis, route)  180 us
    ppermute x36, waiting for transfers between devices, swapped(): return lax.ppermute(value, axis, pairs)  124 us
    unnamed x2, blocking collectives  83.7 us
    scatter-add x6, local copies, waits for them, and re-layouts, backward_micro(): grad_extended.at[:, offset:offset + block_len]  47 us
    ppermute x16, starting transfers between devices, from_behind(): return lax.ppermute(block, axis, route)  41.4 us
    ppermute x36, starting transfers between devices, swapped(): return lax.ppermute(value, axis, pairs)  26.3 us
    another operation x13, other arithmetic  24 us
    another operation x28, local copies, waits for them, and re-layouts  17.9 us
  transfers between devices with their start and end apart: 56, of which 31 were waited for; matrix products, arithmetic and copies ran while one was open for 22% of the time, Pallas kernels for 0%

commit v1 on v0

v1 whole, which is shorter than its diff:
```python
import functools

import jax
import jax.numpy as jnp
from jax import lax
from jax.experimental import pallas as pl
from jax.experimental.pallas import tpu as pltpu
from jax.sharding import PartitionSpec as P

INNER = 1536
HEADS = 24
HDIM = 64
STATE = 128
KCONV = 4
CHANNELS = INNER + 2 * STATE
LANES = 128
CHUNK = 128
HALO = 16
EPSILON = 1e-05
WIDTH = CHANNELS + LANES
SPLIT = 1024
F32 = jnp.float32
BF16 = jnp.bfloat16
BOTH = ("dp", "seq")
VMEM_LIMIT = 60 * 1024 * 1024


def flip_dp(value, mask):
    pairs = [(i, i ^ mask) for i in range(lax.axis_size("dp"))]
    return lax.ppermute(value, "dp", pairs)


def shift_seq(value, step):
    size = lax.axis_size("seq")
    return lax.ppermute(value, "seq", [(i, (i + step) % size) for i in range(size)])


def column_place(dp_even, lin):
    return (dp_even + lin % 2) * lax.axis_size("seq") + lin // 2


def unit_pairs(parity):
    size = lax.axis_size("seq")
    pairs = []
    for dp in range(lax.axis_size("dp")):
        core = dp % 2
        for block in range(size):
            micro = (block % 2) ^ parity
            lin = (2 * micro + core) * (size // 2) + block // 2
            pairs.append((dp * size + block, column_place(dp - core, lin)))
    return pairs


def neighbour_pairs(step):
    size = lax.axis_size("seq")
    group = size // 2
    pairs = []
    for dp_even in range(0, lax.axis_size("dp"), 2):
        for lin in range(2 * size):
            if 0 <= lin % group + step < group:
                pairs.append((column_place(dp_even, lin), column_place(dp_even, lin + step)))
    return pairs


def reversed_pairs(pairs):
    return [(target, source) for source, target in pairs]


def to_stretch(blocks, place):
    odd = place["seq"] % 2 == 1
    late = place["micro"] == 1
    first = lax.ppermute(jnp.where(odd, blocks[1], blocks[0]), BOTH, unit_pairs(0))
    second = lax.ppermute(jnp.where(odd, blocks[0], blocks[1]), BOTH, unit_pairs(1))
    return jnp.where(late, second, first), jnp.where(late, first, second)


def from_stretch(first, second, place):
    odd = place["seq"] % 2 == 1
    late = place["micro"] == 1
    one = lax.ppermute(jnp.where(late, second, first), BOTH, reversed_pairs(unit_pairs(0)))
    two = lax.ppermute(jnp.where(late, first, second), BOTH, reversed_pairs(unit_pairs(1)))
    return jnp.where(odd, two, one), jnp.where(odd, one, two)


def seq_gather(shard, place):
    size = lax.axis_size("seq")
    got = [shard] + [shift_seq(shard, j) for j in range(1, size)]
    rows = []
    for i in range(size):
        row = got[0]
        for j in range(1, size):
            row = jnp.where((place["seq"] - i) % size == j, got[j], row)
        rows.append(row)
    return jnp.stack(rows)


def spread(block, bits):
    masks, held = (0,), block[None]
    last = None
    for bit in bits:
        if last is not None:
            masks, held = masks + last[0], jnp.concatenate([held, last[1]])
        last = (tuple(m ^ (1 << bit) for m in masks), flip_dp(held, 1 << bit))
    pieces = [(masks, held)] + ([last] if last is not None else [])
    return pieces + [(tuple(m ^ 1 for m in part[0]), flip_dp(part[1], 1)) for part in pieces]


def fold(parts, bits):
    order = {bit: i for i, bit in enumerate(sorted(bits, reverse=True))}
    shape = (2,) * len(bits) + parts.shape[1:]
    parts = parts.reshape(shape)
    axes = sorted(bits, reverse=True)
    for bit in bits:
        axis = axes.index(bit)
        axes.pop(axis)
        keep = lax.index_in_dim(parts, 0, axis, keepdims=False)
        give = lax.index_in_dim(parts, 1, axis, keepdims=False).astype(BF16)
        parts = keep + flip_dp(give, 1 << bit).astype(F32)
    del order
    return parts


def seq_scatter(parts, place):
    size = lax.axis_size("seq")
    total = lax.dynamic_index_in_dim(parts, place["seq"], 0, keepdims=False)
    for j in range(1, size):
        give = lax.dynamic_index_in_dim(parts, (place["seq"] + j) % size, 0, keepdims=False)
        total = total + shift_seq(give.astype(BF16), j).astype(F32)
    return total


def sum_everywhere(value):
    for bit in range(lax.axis_size("dp").bit_length() - 1):
        value = value + flip_dp(value, 1 << bit)
    size = lax.axis_size("seq")
    apart = 1
    while apart < size:
        pairs = [(i, i ^ apart) for i in range(size)]
        value = value + lax.ppermute(value, "seq", pairs)
        apart *= 2
    return value


def dp_table(row):
    table = row[None]
    for bit in range(lax.axis_size("dp").bit_length() - 1):
        table = jnp.concatenate([table, flip_dp(table, 1 << bit)])
    return table


def route_kernel(place_ref, table_ref, out_ref):
    dp = place_ref[0]
    size = table_ref.shape[0]
    for way in range(2):
        for micro in range(2):
            first_bit, second_bit = ((2, 4), (4, 2))[micro]
            goal = []
            for r in range(size):
                if way == 1:
                    goal.append(table_ref[r, micro])
                else:
                    found = jnp.int32(0)
                    for other in range(size):
                        hit = table_ref[other, micro] == jnp.bitwise_xor(dp, r)
                        found = jnp.where(hit, jnp.bitwise_xor(dp, other), found)
                    goal.append(found)
            held = [0, 1, first_bit, first_bit | 1]

            def chosen(base):
                low = jnp.int32(0)
                high = jnp.int32(0)
                for n in range(3, -1, -1):
                    away = jnp.bitwise_xor(goal[base ^ held[n]], jnp.bitwise_xor(dp, base))
                    cross = (jnp.bitwise_and(away, second_bit) != 0) & (
                        jnp.bitwise_and(away, first_bit) == 0
                    )
                    low = jnp.where(cross, n, low)
                for n in range(4):
                    away = jnp.bitwise_xor(goal[base ^ held[n]], jnp.bitwise_xor(dp, base))
                    cross = (jnp.bitwise_and(away, second_bit) != 0) & (
                        jnp.bitwise_and(away, first_bit) == 0
                    )
                    high = jnp.where(cross, n, high)
                return low, high

            low, high = chosen(0)
            other_low, _ = chosen(second_bit)
            row = way * 2 + micro
            out_ref[row, 0] = low
            out_ref[row, 1] = high
            for side in range(2):
                pick = jnp.int32(0)
                target = jnp.bitwise_xor(dp, side)
                for n in range(4):
                    pick = jnp.where(goal[held[n]] == target, n, pick)
                    far = jnp.where(other_low == n, 4, 5)
                    pick = jnp.where(goal[held[n] ^ second_bit] == target, far, pick)
                out_ref[row, 2 + side] = pick
    core = jnp.bitwise_and(dp, 1)
    column = jnp.bitwise_xor(core, place_ref[2])
    micro = place_ref[1]
    own = jnp.where(micro == 0, table_ref[0, 2], table_ref[0, 3])
    other = jnp.where(micro == 0, table_ref[1, 2], table_ref[1, 3])
    out_ref[4, 0] = jnp.where(column == 0, own, other)
    for n in range(1, 4):
        out_ref[4, n] = jnp.int32(0)


def make_routes(place, table):
    return pl.pallas_call(
        route_kernel,
        out_shape=jax.ShapeDtypeStruct((5, 4), jnp.int32),
        in_specs=[pl.BlockSpec(memory_space=pltpu.SMEM)] * 2,
        out_specs=pl.BlockSpec(memory_space=pltpu.SMEM),
    )(jnp.stack([place["dp"], place["micro"], place["column"]]), table)


def pick_of(entries, index):
    out = entries[0]
    for n in range(1, len(entries)):
        out = jnp.where(index == n, entries[n], out)
    return out


def deal(items, routes, place):
    low_core = place["dp"] % 2 == 0
    half = items.shape[1] // 2
    top, bottom = items[:, :half], items[:, half:]
    mine = jnp.where(low_core, top, bottom)
    got = flip_dp(jnp.where(low_core, bottom, top), 1)
    own, partner = [], []
    for micro in range(2):
        first_bit, second_bit = ((2, 4), (4, 2))[micro]
        pair = jnp.stack([mine[micro], got[micro]])
        came = flip_dp(pair, first_bit)
        held = [mine[micro], got[micro], came[0], came[1]]
        route = routes[micro]
        sent = jnp.stack([pick_of(held, route[0]), pick_of(held, route[1])])
        far = flip_dp(sent, second_bit)
        held = held + [far[0], far[1]]
        own.append(pick_of(held, route[2]))
        partner.append(pick_of(held, route[3]))
    own = jnp.stack(own)
    back = flip_dp(jnp.stack(partner), 1)
    return jnp.concatenate(
        [jnp.where(low_core, own, back), jnp.where(low_core, back, own)], axis=1
    )


def deal_gathered(items, source):
    every = lax.all_gather(items, "dp", axis=0)
    picked = [
        lax.dynamic_index_in_dim(every[:, m], source[m], 0, keepdims=False) for m in range(2)
    ]
    return jnp.stack(picked)


def dot(a, b, ca=1, cb=0):
    return lax.dot_general(a, b, (((ca,), (cb,)), ((), ())), preferred_element_type=F32)


def two_parts(x):
    high = x.astype(BF16)
    return high, (x - high.astype(F32)).astype(BF16)


def running_sum(x, reverse=False):
    rows = lax.broadcasted_iota(jnp.int32, (CHUNK, CHUNK), 0)
    cols = lax.broadcasted_iota(jnp.int32, (CHUNK, CHUNK), 1)
    reach = (rows <= cols) if reverse else (rows >= cols)
    reach = jnp.where(reach, 1.0, 0.0).astype(BF16)
    high, rest = two_parts(x)
    middle, low = two_parts(x - high.astype(F32))
    del rest
    return dot(reach, high) + dot(reach, middle) + dot(reach, low)


def fill_expander(expand_ref):
    head = lax.broadcasted_iota(jnp.int32, (LANES, INNER), 0)
    col = lax.broadcasted_iota(jnp.int32, (LANES, INNER), 1)
    one = jnp.where(col // HDIM == head, 1.0, 0.0).astype(BF16)
    expand_ref[0:LANES, :] = one
    expand_ref[LANES : 2 * LANES, :] = one


def head_sums(prod, tile):
    lane = lax.broadcasted_iota(jnp.int32, (LANES, LANES), 0)
    head = lax.broadcasted_iota(jnp.int32, (LANES, LANES), 1)
    one = jnp.where(2 * tile + lane // HDIM == head, 1.0, 0.0).astype(BF16)
    high, low = two_parts(prod)
    return dot(jnp.concatenate([high, low], axis=1), jnp.concatenate([one, one], axis=0))


def start_pieces(dp, pieces, plan, target, sem, rows):
    copies = []
    for piece, (masks, spots) in zip(pieces, plan):
        for n, mask in enumerate(masks):
            for source, scale, col, width in spots:
                first = pl.multiple_of(jnp.bitwise_xor(dp, mask) * (rows * scale), 8)
                copy = pltpu.make_async_copy(
                    piece.at[n, pl.ds(source, rows * scale), :],
                    target.at[pl.ds(first, rows * scale), pl.ds(col, width)],
                    sem.at[len(copies)],
                )
                copy.start()
                copies.append(copy)
    return copies


def wait_all(copies):
    for copy in copies:
        copy.wait()


def piece_count(plan):
    return sum(len(masks) * len(spots) for masks, spots in plan)


def gain_row(w_ref):
    return w_ref[:, CHANNELS:].astype(F32).T[HEADS : HEADS + 1]


def project_kernel(plan, rows, scal, x_ref, cw_ref, cb_ref, dl_ref, sb_ref, *refs):
    count = len(plan)
    pieces = refs[:count]
    nh_ref, cext_ref, act_ref, step_ref, sig_ref, cum_ref, upd_ref, tot_ref = refs[count : count + 8]
    w_ref, proj_ref, expand_ref, sem = refs[count + 8 :]
    copies = start_pieces(scal[0], pieces, plan, w_ref, sem, rows)
    total = x_ref.shape[0]
    length = total - HALO
    chunks = length // CHUNK
    fill_expander(expand_ref)

    def norm(i, carry):
        at = pl.ds(pl.multiple_of(i * HALO, HALO), HALO)
        u = x_ref[at, :].astype(F32)
        scale = lax.rsqrt(jnp.mean(u * u, axis=1, keepdims=True) + EPSILON)
        nh_ref[at, :] = (u * scale * gain).astype(BF16)
        return carry

    wait_all(copies)
    gain = gain_row(w_ref)
    lax.fori_loop(0, total // HALO, norm, 0)

    def project(j, carry):
        at = pl.ds(pl.multiple_of(j * 384, 384), 384)
        proj_ref[:, at] = dot(nh_ref[...], w_ref[:, at])
        return carry

    lax.fori_loop(0, WIDTH // 384, project, 0)

    def conv(idx, carry):
        i, j = idx // (CHANNELS // LANES), idx % (CHANNELS // LANES)
        cols = pl.ds(pl.multiple_of(j * LANES, LANES), LANES)
        first = pl.multiple_of(i * CHUNK, CHUNK)
        part = proj_ref[pl.ds(first, CHUNK + HALO), cols]
        weights = cw_ref[:, cols]
        out = cb_ref[0:1, cols] + weights[KCONV - 1 : KCONV] * part[HALO:]
        for k in range(KCONV - 1):
            out = out + weights[k : k + 1] * pltpu.roll(part, KCONV - 1 - k, 0)[HALO:]
        act_ref[pl.ds(first, CHUNK), cols] = (out * jax.nn.sigmoid(out)).astype(BF16)
        cext_ref[pl.ds(first + HALO, CHUNK), cols] = part[HALO:].astype(BF16)
        return carry

    lax.fori_loop(0, chunks * (CHANNELS // LANES), conv, 0)
    cext_ref[0:HALO, :] = proj_ref[0:HALO, 0:CHANNELS].astype(BF16)
    lane = lax.broadcasted_iota(jnp.int32, (CHUNK, LANES), 1)
    row = lax.broadcasted_iota(jnp.int32, (CHUNK, LANES), 0)
    rate = -jnp.exp(dl_ref[0:1, :])
    lasts = []
    for i in range(chunks):
        at = pl.ds(i * CHUNK, CHUNK)
        pre = proj_ref[pl.ds(HALO + i * CHUNK, CHUNK), pl.ds(CHANNELS, LANES)] + sb_ref[0:1, :]
        live = (row + i * CHUNK < scal[1]) & (lane < HEADS)
        soft = jnp.maximum(pre, 0.0) + jnp.log1p(jnp.exp(-jnp.abs(pre)))
        step = jnp.where(live, soft, 0.0)
        step_ref[at, :] = step
        sig_ref[at, :] = jnp.where(live, jax.nn.sigmoid(pre), 0.0)
        cum = running_sum(rate * step)
        cum_ref[at, :] = cum
        lasts.append(cum[CHUNK - 1 : CHUNK])
    after = jnp.zeros_like(lasts[0])
    for i in range(chunks - 1, -1, -1):
        at = pl.ds(i * CHUNK, CHUNK)
        weight = jnp.exp(lasts[i] + after - cum_ref[at, :]) * step_ref[at, :]
        wide = dot(jnp.concatenate(two_parts(weight), axis=1), expand_ref[...])
        values = act_ref[at, 0:INNER].astype(F32)
        keys = act_ref[at, INNER : INNER + STATE]
        update = dot(keys, (wide * values).astype(BF16), 0, 0)
        proj_ref[0:STATE, 0:INNER] = (
            update if i == chunks - 1 else proj_ref[0:STATE, 0:INNER] + update
        )
        after = after + lasts[i]
    upd_ref[...] = proj_ref[0:STATE, 0:INNER].astype(BF16)
    tot_ref[...] = jnp.broadcast_to(after, tot_ref.shape)


def mixing_parts(cum, cum_rows, step_rows, head):
    gap = jnp.minimum(cum[:, head : head + 1] - cum_rows[head : head + 1, :], 0.0)
    return jnp.exp(gap) * step_rows[head : head + 1, :]


def causal_tile():
    rows = lax.broadcasted_iota(jnp.int32, (CHUNK, CHUNK), 0)
    cols = lax.broadcasted_iota(jnp.int32, (CHUNK, CHUNK), 1)
    return rows >= cols


def local_kernel(plan, rows, scal, nh_ref, act_ref, step_ref, cum_ref, *refs):
    count = len(plan)
    pieces = refs[:count]
    local_ref, gate_ref, w_ref, sem = refs[count:]
    copies = start_pieces(scal[0], pieces, plan, w_ref, sem, rows)
    chunks = act_ref.shape[0] // CHUNK
    left = lax.broadcasted_iota(jnp.int32, (CHUNK, LANES), 1) < HDIM

    def chunk(c, carry):
        at = pl.ds(pl.multiple_of(c * CHUNK, CHUNK), CHUNK)
        in_keys = act_ref[at, INNER : INNER + STATE]
        out_keys = act_ref[at, INNER + STATE : CHANNELS]
        affinity = jnp.where(causal_tile(), dot(out_keys, in_keys, 1, 1), 0.0)
        cum = cum_ref[at, :]
        cum_rows = cum.T
        step_rows = step_ref[at, :].T
        for tile in range(INNER // LANES):
            cols = slice(tile * LANES, (tile + 1) * LANES)
            mixing = [
                (affinity * mixing_parts(cum, cum_rows, step_rows, 2 * tile + n)).astype(BF16)
                for n in range(2)
            ]
            values = act_ref[at, cols]
            zero = jnp.zeros_like(values)
            apart = jnp.concatenate(
                [jnp.where(left, values, zero), jnp.where(left, zero, values)], axis=0
            )
            local_ref[at, cols] = dot(jnp.concatenate(mixing, axis=1), apart)
        return carry

    lax.fori_loop(0, chunks, chunk, 0)
    wait_all(copies)

    def project(j, carry):
        at = pl.ds(pl.multiple_of(j * 384, 384), 384)
        gate_ref[:, at] = dot(nh_ref[HALO:, :], w_ref[:, at])
        return carry

    lax.fori_loop(0, INNER // 384, project, 0)


def middle_kernel(plan, rows, scal, local_ref, act_ref, step_ref, cum_ref, gate_ref, state_ref, x_ref, c_ref,
                  skip_ref, *refs):
    count = len(plan)
    pieces = refs[:count]
    out_ref, gn_ref, dgate_ref, gcore_ref, rowq_ref, lsg_ref, states_ref, gskip_ref = refs[
        count : count + 8
    ]
    w_ref, gain_ref, mc_ref, gno_ref, state_s, wide_ref, core_ref, mixed_ref, acc_ref, expand_ref, sem = refs[
        count + 8 :
    ]
    copies = start_pieces(scal[0], pieces, plan, w_ref, sem, rows)
    length = act_ref.shape[0]
    chunks = length // CHUNK
    tiles = INNER // LANES
    model = c_ref.shape[1]
    fill_expander(expand_ref)

    def mask(i, carry):
        at = pl.ds(pl.multiple_of(i * CHUNK, CHUNK), CHUNK)
        row = lax.broadcasted_iota(jnp.int32, (CHUNK, model), 0) + i * CHUNK
        c = c_ref[at, :]
        mc_ref[at, :] = jnp.where(row < scal[1], c.astype(F32), 0.0).astype(BF16)
        return carry

    lax.fori_loop(0, chunks, mask, 0)
    wait_all(copies)

    def back_project(j, carry):
        at = pl.ds(pl.multiple_of(j * 384, 384), 384)
        gno_ref[:, at] = dot(mc_ref[...], w_ref[at, 0:model], 1, 1)
        return carry

    lax.fori_loop(0, INNER // 384, back_project, 0)
    gain_ref[...] = w_ref[:, model:].astype(F32).T[0:8]
    state_s[...] = state_ref[...].astype(F32)
    acc_ref[...] = jnp.zeros_like(acc_ref)
    gskip_ref[...] = jnp.zeros_like(gskip_ref)

    def chunk(c, before):
        at = pl.ds(pl.multiple_of(c * CHUNK, CHUNK), CHUNK)
        in_keys = act_ref[at, INNER : INNER + STATE]
        out_keys = act_ref[at, INNER + STATE : CHANNELS]
        cum = cum_ref[at, :]
        last = cum[CHUNK - 1 : CHUNK]
        growth = jnp.exp(cum)
        weight = jnp.exp(last - cum) * step_ref[at, :]
        small = jnp.concatenate(
            [growth, weight, jnp.exp(cum + before), jnp.broadcast_to(jnp.exp(last), (8, LANES))], axis=0
        )
        wide_ref[...] = dot(jnp.concatenate(two_parts(small), axis=1), expand_ref[...])
        state_b = state_s[...].astype(BF16)
        states_ref[c] = state_b
        squares = jnp.zeros((CHUNK, LANES), F32)
        for tile in range(tiles):
            cols = slice(tile * LANES, (tile + 1) * LANES)
            values = act_ref[at, cols].astype(F32)
            readout = dot(out_keys, state_b[:, cols])
            core = local_ref[at, cols] + wide_ref[0:CHUNK, cols] * readout
            mixed = core + skip_ref[0:1, cols] * values
            core_ref[:, cols] = core
            mixed_ref[:, cols] = mixed
            gate = gate_ref[at, cols]
            gated = mixed * (gate * jax.nn.sigmoid(gate))
            squares = squares + gated * gated
            weighted = (wide_ref[CHUNK : 2 * CHUNK, cols] * values).astype(BF16)
            state_s[:, cols] = wide_ref[3 * CHUNK : 3 * CHUNK + 1, cols] * state_s[:, cols] + dot(
                in_keys, weighted, 0, 0
            )
        scale = lax.rsqrt(jnp.sum(squares, axis=1, keepdims=True) / INNER + EPSILON)
        products = jnp.zeros((CHUNK, LANES), F32)
        for tile in range(tiles):
            cols = slice(tile * LANES, (tile + 1) * LANES)
            gate = gate_ref[at, cols]
            gn = mixed_ref[:, cols] * (gate * jax.nn.sigmoid(gate)) * scale
            gain = gain_ref[0:1, cols]
            gn_ref[at, cols] = (gn * gain).astype(BF16)
            products = products + gn * (gno_ref[at, cols] * gain)
        mean = jnp.sum(products, axis=1, keepdims=True) / INNER
        rowq = jnp.zeros((CHUNK, LANES), F32)
        for tile in range(tiles):
            cols = slice(tile * LANES, (tile + 1) * LANES)
            gate = gate_ref[at, cols]
            sig = jax.nn.sigmoid(gate)
            silu = gate * sig
            mixed = mixed_ref[:, cols]
            dgated = scale * (gno_ref[at, cols] * gain_ref[0:1, cols] - (mixed * silu * scale) * mean)
            g = dgated * silu
            dgate_ref[at, cols] = (dgated * mixed * (sig * (1.0 + gate * (1.0 - sig)))).astype(BF16)
            gcore = g.astype(BF16)
            gcore_ref[at, cols] = gcore
            values = act_ref[at, cols].astype(F32)
            gskip_ref[:, cols] = gskip_ref[:, cols] + jnp.sum(
                (g * values).reshape(CHUNK // 8, 8, LANES), axis=0
            )
            gcore_f = gcore.astype(F32)
            rowq = rowq + head_sums(gcore_f * core_ref[:, cols], tile)
            scaled = (wide_ref[2 * CHUNK : 3 * CHUNK, cols] * gcore_f).astype(BF16)
            acc_ref[:, cols] = acc_ref[:, cols] + dot(out_keys, scaled, 0, 0)
        rowq_ref[at, :] = rowq
        return before + last

    lax.fori_loop(0, chunks, chunk, jnp.zeros((1, LANES), F32))
    lsg_ref[...] = acc_ref[...].astype(BF16)

    def finish(i, carry):
        at = pl.ds(pl.multiple_of(i * CHUNK, CHUNK), CHUNK)
        row = lax.broadcasted_iota(jnp.int32, (CHUNK, model), 0) + i * CHUNK
        u = x_ref[pl.ds(pl.multiple_of(i * CHUNK + HALO, HALO), CHUNK), :].astype(F32)
        out_ref[at, :] = (u + jnp.where(row < scal[1], gno_ref[at, 0:model], 0.0)).astype(BF16)
        return carry

    for j in range(2):
        cols = slice(j * model // 2, (j + 1) * model // 2)
        gno_ref[:, cols] = dot(gn_ref[...], w_ref[:, cols])
    lax.fori_loop(0, chunks, finish, 0)


def put_block(dp, block, keep_ref, send_ref, start, cols, part):
    away = jnp.bitwise_xor(dp, block)
    slot = away // 2
    rows = part.shape[0]

    @pl.when(away % 2 == 0)
    def _():
        keep_ref[slot, start : start + rows, cols] = part

    @pl.when(away % 2 == 1)
    def _():
        send_ref[slot, start : start + rows, cols] = part


def early_kernel(plan, rows, devices, scal, act_ref, step_ref, cum_ref, gcore_ref, gn_ref, c_ref, nh_ref,
                 dgate_ref, *refs):
    count = len(plan)
    pieces = refs[:count]
    gvl_ref, gk_ref, gng_ref, keep_ref, send_ref = refs[count : count + 5]
    w_ref, mc_ref, sem = refs[count + 5 :]
    copies = start_pieces(scal[0], pieces, plan, w_ref, sem, rows)
    length, model = c_ref.shape
    chunks = length // CHUNK
    left = lax.broadcasted_iota(jnp.int32, (CHUNK, LANES), 1) < HDIM

    def mask(i, carry):
        at = pl.ds(pl.multiple_of(i * CHUNK, CHUNK), CHUNK)
        row = lax.broadcasted_iota(jnp.int32, (CHUNK, model), 0) + i * CHUNK
        mc_ref[at, :] = jnp.where(row < scal[1], c_ref[at, :].astype(F32), 0.0).astype(BF16)
        return carry

    lax.fori_loop(0, chunks, mask, 0)
    half = model // 2
    for j in range(2 * INNER // model):
        part = dot(nh_ref[HALO:, :], dgate_ref[:, j * half : (j + 1) * half], 0, 0).astype(BF16)
        start = (j // 2) * rows
        cols = slice((j % 2) * half, (j % 2 + 1) * half)
        for block in range(devices):
            put_block(
                scal[0], block, keep_ref, send_ref, start, cols, part[block * rows : (block + 1) * rows]
            )
    for j in range(INNER // half):
        part = dot(gn_ref[:, j * half : (j + 1) * half], mc_ref[...], 0, 0).astype(BF16)
        each = half // (2 * rows)
        for n in range(each):
            put_block(
                scal[0], j * each + n, keep_ref, send_ref, 2 * rows, slice(0, model),
                part[n * 2 * rows : (n + 1) * 2 * rows],
            )

    def chunk(c, carry):
        at = pl.ds(pl.multiple_of(c * CHUNK, CHUNK), CHUNK)
        in_keys = act_ref[at, INNER : INNER + STATE]
        out_keys = act_ref[at, INNER + STATE : CHANNELS]
        affinity = jnp.where(causal_tile(), dot(out_keys, in_keys, 1, 1), 0.0)
        cum = cum_ref[at, :]
        cum_rows = cum.T
        step_rows = step_ref[at, :].T
        gaff = jnp.zeros((CHUNK, CHUNK), F32)
        for tile in range(INNER // LANES):
            cols = slice(tile * LANES, (tile + 1) * LANES)
            values = act_ref[at, cols]
            grads = gcore_ref[at, cols]
            zero = jnp.zeros_like(grads)
            apart = jnp.concatenate(
                [jnp.where(left, grads, zero), jnp.where(left, zero, grads)], axis=0
            )
            gmix = dot(apart, values, 1, 1)
            mixing = []
            for n in range(2):
                weight = mixing_parts(cum, cum_rows, step_rows, 2 * tile + n)
                gaff = gaff + gmix[n * CHUNK : (n + 1) * CHUNK] * weight
                mixing.append((affinity * weight).astype(BF16))
            back = dot(jnp.concatenate(mixing, axis=1), grads, 0, 0)
            gvl_ref[at, cols] = jnp.where(left, back[0:CHUNK], back[CHUNK:])
        gaff = jnp.where(causal_tile(), gaff, 0.0).astype(BF16)
        gk_ref[at, 0:STATE] = dot(gaff, out_keys, 0, 0)
        gk_ref[at, STATE : 2 * STATE] = dot(gaff, in_keys)
        return carry

    lax.fori_loop(0, chunks, chunk, 0)
    wait_all(copies)
    for j in range(2):
        cols = slice(j * half, (j + 1) * half)
        gng_ref[:, cols] = dot(dgate_ref[...], w_ref[cols, :], 1, 1)


def late_kernel(plan, rows, devices, scal, act_ref, step_ref, sig_ref, cum_ref, gcore_ref, gvl_ref, gk_ref,
                gng_ref, rowq_ref, states_ref, gout_ref, gskip_ref, skip_ref, x_ref, c_ref, nh_ref,
                cext_ref, cw_ref, cb_ref, dl_ref, *refs):
    count = len(plan)
    pieces = refs[:count]
    gtok_ref, last_ref, ghalo_ref, keep_ref, send_ref, small_ref = refs[count : count + 6]
    w_ref, gstate_ref, wide_ref, gact_ref, gpad_ref, gproj_ref, acc_ref, expand_ref, sem = refs[
        count + 6 :
    ]
    copies = start_pieces(scal[0], pieces, plan, w_ref, sem, rows)
    length, model = c_ref.shape
    chunks = length // CHUNK
    tiles = INNER // LANES
    fill_expander(expand_ref)
    gstate_ref[...] = gout_ref[...].astype(F32)
    small_ref[...] = jnp.zeros_like(small_ref)
    small_ref[6:7, 0:INNER] = jnp.sum(gskip_ref[...], axis=0, keepdims=True)
    gpad_ref[0:HALO, :] = jnp.zeros((HALO, CHANNELS), F32)
    gpad_ref[HALO + length :, :] = jnp.zeros((HALO, CHANNELS), F32)
    gproj_ref[0:HALO, CHANNELS:] = jnp.zeros((HALO, LANES), BF16)
    rate = -jnp.exp(dl_ref[0:1, :])
    end = lax.broadcasted_iota(jnp.int32, (CHUNK, LANES), 0) == CHUNK - 1

    def chunk(n, carry):
        gdecay, gbias = carry
        c = chunks - 1 - n
        at = pl.ds(pl.multiple_of(c * CHUNK, CHUNK), CHUNK)
        in_keys = act_ref[at, INNER : INNER + STATE]
        out_keys = act_ref[at, INNER + STATE : CHANNELS]
        cum = cum_ref[at, :]
        step = step_ref[at, :]
        sig = sig_ref[at, :]
        last = cum[CHUNK - 1 : CHUNK]
        small = jnp.concatenate(
            [jnp.exp(cum), jnp.exp(last - cum) * step, jnp.broadcast_to(jnp.exp(last), (8, LANES))], axis=0
        )
        wide_ref[...] = dot(jnp.concatenate(two_parts(small), axis=1), expand_ref[...])
        colq = jnp.zeros((CHUNK, LANES), F32)
        ends = jnp.zeros((8, LANES), F32)
        gin = gk_ref[at, 0:STATE]
        gout = gk_ref[at, STATE : 2 * STATE]
        for tile in range(tiles):
            cols = slice(tile * LANES, (tile + 1) * LANES)
            values = act_ref[at, cols].astype(F32)
            grads = gcore_ref[at, cols].astype(F32)
            gstate = gstate_ref[:, cols]
            gstate_b = gstate.astype(BF16)
            state = states_ref[c, :, cols]
            weight = wide_ref[CHUNK : 2 * CHUNK, cols]
            decay = wide_ref[2 * CHUNK : 2 * CHUNK + 1, cols]
            gvs = weight * dot(in_keys, gstate_b)
            gvalues = gvl_ref[at, cols] + gvs
            colq = colq + head_sums(values * gvalues, tile)
            passed = jnp.sum((values * gvs).reshape(CHUNK // 8, 8, LANES), axis=0) + decay * jnp.sum(
                (gstate * state.astype(F32)).reshape(STATE // 8, 8, LANES), axis=0
            )
            ends = ends + head_sums(passed, tile)
            gin = gin + dot((weight * values).astype(BF16), gstate_b, 1, 1)
            scaled = (wide_ref[0:CHUNK, cols] * grads).astype(BF16)
            gout = gout + dot(scaled, state, 1, 1)
            gstate_ref[:, cols] = decay * gstate + dot(out_keys, scaled, 0, 0)
            gact_ref[:, cols] = gvalues + skip_ref[0:1, cols] * grads
        gact_ref[:, INNER : INNER + STATE] = gin
        gact_ref[:, INNER + STATE : CHANNELS] = gout
        gcum = rowq_ref[at, :] - colq
        gcum = gcum + jnp.where(end, jnp.sum(ends, axis=0, keepdims=True), 0.0)
        glog = running_sum(gcum, reverse=True)
        gdecay = gdecay + jnp.sum((glog * (rate * step)).reshape(CHUNK // 8, 8, LANES), axis=0)
        ratio = jnp.where(step > 0.0, sig / jnp.where(step > 0.0, step, 1.0), 0.0)
        graw = colq * ratio + rate * glog * sig
        gbias = gbias + jnp.sum(graw.reshape(CHUNK // 8, 8, LANES), axis=0)
        first = pl.multiple_of(c * CHUNK, CHUNK)
        gproj_ref[pl.ds(first + HALO, CHUNK), CHANNELS:] = graw.astype(BF16)
        for tile in range(CHANNELS // LANES):
            cols = slice(tile * LANES, (tile + 1) * LANES)
            part = cext_ref[pl.ds(first, CHUNK + HALO), cols].astype(F32)
            moved = [pltpu.roll(part, KCONV - 1 - k, 0)[HALO:] for k in range(KCONV - 1)] + [part[HALO:]]
            out = cb_ref[0:1, cols]
            for k in range(KCONV):
                out = out + cw_ref[k : k + 1, cols] * moved[k]
            sc = jax.nn.sigmoid(out)
            gconv = gact_ref[:, cols] * (sc * (1.0 + out * (1.0 - sc)))
            gpad_ref[pl.ds(first + HALO, CHUNK), cols] = gconv
            for k in range(KCONV):
                small_ref[k : k + 1, cols] = small_ref[k : k + 1, cols] + jnp.sum(
                    gconv * moved[k], axis=0, keepdims=True
                )
            small_ref[4:5, cols] = small_ref[4:5, cols] + jnp.sum(gconv, axis=0, keepdims=True)
        return gdecay, gbias

    zero = jnp.zeros((8, LANES), F32)
    gdecay, gbias = lax.fori_loop(0, chunks, chunk, (zero, zero))
    small_ref[5:6, 0:LANES] = jnp.sum(gdecay, axis=0, keepdims=True)
    small_ref[5:6, LANES : 2 * LANES] = jnp.sum(gbias, axis=0, keepdims=True)

    def conv_back(i, carry):
        first = pl.multiple_of(i * HALO, HALO)
        for tile in range(CHANNELS // LANES):
            cols = slice(tile * LANES, (tile + 1) * LANES)
            part = gpad_ref[pl.ds(first, 2 * HALO), cols]
            total = cw_ref[KCONV - 1 : KCONV, cols] * part[:HALO]
            for k in range(KCONV - 1):
                ahead = pltpu.roll(part, 2 * HALO - (KCONV - 1 - k), 0)[:HALO]
                total = total + cw_ref[k : k + 1, cols] * ahead
            gproj_ref[pl.ds(first, HALO), cols] = total.astype(BF16)
        return carry

    lax.fori_loop(0, (length + HALO) // HALO, conv_back, 0)
    for j in range(WIDTH // 384):
        cols = slice(j * 384, (j + 1) * 384)
        part = dot(nh_ref[...], gproj_ref[:, cols], 0, 0).astype(BF16)
        for block in range(devices):
            put_block(
                scal[0], block, keep_ref, send_ref, 0, cols, part[block * rows : (block + 1) * rows]
            )
    wait_all(copies)
    for j in range(2):
        cols = slice(j * model // 2, (j + 1) * model // 2)
        acc_ref[:, cols] = dot(gproj_ref[...], w_ref[cols, :], 1, 1)
    acc_ref[HALO:, :] = acc_ref[HALO:, :] + gng_ref[...]
    gain = gain_row(w_ref)

    def norm_back(i, carry):
        at = pl.ds(pl.multiple_of(i * HALO, HALO), HALO)
        u = x_ref[at, :].astype(F32)
        scale = lax.rsqrt(jnp.mean(u * u, axis=1, keepdims=True) + EPSILON)
        nh = u * scale
        g = acc_ref[at, :] * gain
        acc_ref[at, :] = scale * (g - nh * jnp.mean(g * nh, axis=1, keepdims=True))
        return carry

    lax.fori_loop(0, (length + HALO) // HALO, norm_back, 0)
    ghalo_ref[...] = acc_ref[0:HALO, :]
    last_ref[...] = acc_ref[length:, :] + c_ref[length - HALO :, :].astype(F32)

    def finish(i, carry):
        at = pl.ds(pl.multiple_of(i * HALO, HALO), HALO)
        grads = acc_ref[pl.ds(pl.multiple_of((i + 1) * HALO, HALO), HALO), :]
        gtok_ref[at, :] = (grads + c_ref[at, :].astype(F32)).astype(BF16)
        return carry

    lax.fori_loop(0, length // HALO, finish, 0)


def call(body, scal, whole, pieces, outs, scratch):
    smem = pl.BlockSpec(memory_space=pltpu.SMEM)
    vmem = pl.BlockSpec(memory_space=pltpu.VMEM)
    return pl.pallas_call(
        body,
        out_shape=[jax.ShapeDtypeStruct(shape, kind) for shape, kind in outs],
        in_specs=[smem] + [vmem] * len(whole) + [pl.BlockSpec(memory_space=pl.ANY)] * len(pieces),
        out_specs=[vmem] * len(outs),
        scratch_shapes=scratch,
        compiler_params=pltpu.CompilerParams(vmem_limit_bytes=VMEM_LIMIT),
    )(scal, *whole, *pieces)


def lane_row(vector):
    return jnp.pad(vector, (0, LANES - vector.shape[0]))[None]


def per_device(tokens, lengths, dealing, cotangent, in_weight, out_weight, norm_gain, gate_gain, conv_weight,
               conv_bias, decay_log, step_bias, skip_gain):
    dp, seq = lax.axis_index("dp"), lax.axis_index("seq")
    devices, size = lax.axis_size("dp"), lax.axis_size("seq")
    group = size // 2
    lin = seq * 2 + dp % 2
    holder = lin // group
    place = {"dp": dp, "seq": seq, "micro": holder // 2, "column": holder % 2, "turn": lin % group}
    block_len, model = tokens.shape[2:]
    length = 2 * block_len
    shard_rows = in_weight.shape[0]
    rows = shard_rows * size
    bits = list(range(1, devices.bit_length() - 1))
    tok = tokens[:, 0]
    cot = cotangent[:, 0]

    gains = jnp.concatenate(
        [norm_gain[:, None], jnp.swapaxes(gate_gain.reshape(2, shard_rows), 0, 1)], axis=1
    )
    conv_shard = jnp.concatenate([in_weight[:, INNER:], gains], axis=1)
    conv_shard = jnp.pad(conv_shard, ((0, 0), (0, WIDTH - conv_shard.shape[1])))
    rest_shard = jnp.concatenate([in_weight[:, :model], in_weight[:, model:INNER], out_weight], axis=0)
    conv_z = seq_gather(conv_shard, place)
    conv_block = conv_z.reshape(rows, WIDTH)
    gate_gains = jnp.swapaxes(conv_z[:, :, CHANNELS + HEADS + 1 : CHANNELS + HEADS + 3], 1, 2)
    gate_gains = jnp.pad(gate_gains.reshape(2 * rows, 1), ((0, 0), (0, LANES - 1)))
    conv_a = spread(conv_block[:, :SPLIT], bits)
    conv_b = spread(conv_block[:, SPLIT:], bits[::-1])
    rest_block = seq_gather(rest_shard, place)
    gate_block = jnp.swapaxes(rest_block[:, : 2 * shard_rows].reshape(size, 2, shard_rows, model), 0, 1)
    gate_p = spread(gate_block.reshape(2 * rows, model), bits)
    out_block = jnp.concatenate([rest_block[:, 2 * shard_rows :].reshape(2 * rows, model), gate_gains], axis=1)
    out_p = spread(out_block, bits[::-1])
    conv_pieces = [part for _, part in conv_a + conv_b]
    conv_plan = [(masks, [(0, 1, 0, SPLIT)]) for masks, _ in conv_a] + [
        (masks, [(0, 1, SPLIT, WIDTH - SPLIT)]) for masks, _ in conv_b
    ]
    gate_pieces = [part for _, part in gate_p]
    gate_plan = [(masks, [(0, 1, 0, model), (rows, 1, model, model)]) for masks, _ in gate_p]
    out_pieces = [part for _, part in out_p]
    out_plan = [(masks, [(0, 2, 0, model + LANES)]) for masks, _ in out_p]

    if devices == 8:
        table = dp_table(jnp.concatenate([dealing[:, 0], lengths[:, 0]]))
        routes = make_routes(place, table)
        own_length = routes[4, 0]
        cot_given = deal(cot, routes[0:2], place)
    else:
        every = lax.all_gather(jnp.concatenate([dealing, lengths], axis=0)[:, 0], "dp", axis=0)
        goals = every[:, :2]
        source_of_out = jnp.argmax(goals == dp, axis=0)
        cot_given = deal_gathered(cot, dealing[:, 0])
        mate = lax.dynamic_index_in_dim(every, dp - dp % 2 + place["column"], 0, keepdims=False)
        own_length = jnp.where(place["micro"] == 0, mate[2], mate[3])
    n_valid = jnp.clip(own_length - place["turn"] * length, 0, length)
    scal = jnp.stack([dp, n_valid])

    first, second = to_stretch(tok, place)
    halo = lax.ppermute(second[block_len - HALO :], BOTH, neighbour_pairs(1))
    x_ext = jnp.concatenate([halo, first, second])
    c_own = jnp.concatenate(to_stretch(cot_given, place))

    taps = jnp.pad(conv_weight, ((0, 8 - KCONV), (0, 0)))
    conv_bias_row = conv_bias[None]
    decay_row, bias_row = lane_row(decay_log), lane_row(step_bias)
    skip_row = jnp.repeat(skip_gain, HDIM)[None]

    def sems(plan):
        return pltpu.SemaphoreType.DMA((piece_count(plan),))

    wide = (length, INNER)
    nh, cext, act, step, sig, cum, update, total = call(
        functools.partial(project_kernel, conv_plan, rows),
        scal,
        [x_ext, taps, conv_bias_row, decay_row, bias_row],
        conv_pieces,
        [((length + HALO, model), BF16), ((length + HALO, CHANNELS), BF16), ((length, CHANNELS), BF16)]
        + [((length, LANES), F32)] * 3 + [((STATE, INNER), BF16), ((8, LANES), F32)],
        [pltpu.VMEM((model, WIDTH), BF16), pltpu.VMEM((length + HALO, WIDTH), F32),
         pltpu.VMEM((2 * LANES, INNER), BF16), sems(conv_plan)],
    )
    passing = jnp.repeat(jnp.exp(total[0, :HEADS]), HDIM)[None] if group > 2 else None

    def relay(own, pairs):
        carried = None
        for _ in range(group - 1):
            given = own if carried is None else (passing * carried.astype(F32) + own.astype(F32)).astype(BF16)
            carried = lax.ppermute(given, BOTH, pairs)
        return jnp.zeros_like(own) if carried is None else carried

    state_in = relay(update, neighbour_pairs(1))
    local, gate = call(
        functools.partial(local_kernel, gate_plan, rows),
        scal,
        [nh, act, step, cum],
        gate_pieces,
        [(wide, F32), (wide, F32)],
        [pltpu.VMEM((model, INNER), BF16), sems(gate_plan)],
    )
    out, gn, dgate, gcore, rowq, lsg, states, gskip = call(
        functools.partial(middle_kernel, out_plan, rows),
        scal,
        [local, act, step, cum, gate, state_in, x_ext, c_own, skip_row],
        out_pieces,
        [((length, model), BF16), (wide, BF16), (wide, BF16), (wide, BF16), ((length, LANES), F32),
         ((STATE, INNER), BF16), ((length // CHUNK, STATE, INNER), BF16), ((8, INNER), F32)],
        [pltpu.VMEM((INNER, model + LANES), BF16), pltpu.VMEM((8, INNER), F32),
         pltpu.VMEM((length, model), BF16), pltpu.VMEM(wide, F32), pltpu.VMEM((STATE, INNER), F32), pltpu.VMEM((3 * CHUNK + 8, INNER), F32),
         pltpu.VMEM((CHUNK, INNER), F32), pltpu.VMEM((CHUNK, INNER), F32), pltpu.VMEM((STATE, INNER), F32),
         pltpu.VMEM((2 * LANES, INNER), BF16), sems(out_plan)],
    )
    grad_out_state = relay(lsg, neighbour_pairs(-1))
    half_dp = devices // 2
    gvl, gk, gng, keep1, send1 = call(
        functools.partial(early_kernel, gate_plan, rows, devices),
        scal,
        [act, step, cum, gcore, gn, c_own, nh, dgate],
        gate_pieces,
        [(wide, F32), ((length, 2 * STATE), F32), ((length, model), F32)]
        + [((half_dp, 4 * rows, model), BF16)] * 2,
        [pltpu.VMEM((model, INNER), BF16), pltpu.VMEM((length, model), BF16), sems(gate_plan)],
    )
    gtok, last, ghalo, keep2, send2, small = call(
        functools.partial(late_kernel, conv_plan, rows, devices),
        scal,
        [act, step, sig, cum, gcore, gvl, gk, gng, rowq, states, grad_out_state, gskip, skip_row, x_ext,
         c_own, nh, cext, taps, conv_bias_row, decay_row],
        conv_pieces,
        [((length, model), BF16), ((HALO, model), F32), ((HALO, model), F32)]
        + [((half_dp, rows, WIDTH), BF16)] * 2 + [((8, WIDTH), F32)],
        [pltpu.VMEM((model, WIDTH), BF16), pltpu.VMEM((STATE, INNER), F32),
         pltpu.VMEM((2 * CHUNK + 8, INNER), F32), pltpu.VMEM((CHUNK, CHANNELS), F32),
         pltpu.VMEM((length + 2 * HALO, CHANNELS), F32), pltpu.VMEM((length + HALO, WIDTH), BF16),
         pltpu.VMEM((length + HALO, model), F32), pltpu.VMEM((2 * LANES, INNER), BF16), sems(conv_plan)],
    )

    out_blocks = jnp.stack(from_stretch(out[:block_len], out[block_len:], place))
    if devices == 8:
        outputs = deal(out_blocks, routes[2:4], place)
    else:
        outputs = deal_gathered(out_blocks, source_of_out)

    early = keep1.astype(F32) + flip_dp(send1, 1).astype(F32)
    early_gate = fold(early[:, : 2 * rows], bits[::-1]).reshape(2, size, shard_rows, model)
    early_out = fold(early[:, 2 * rows :], bits).reshape(size, 2 * shard_rows, model)
    early_all = jnp.concatenate([early_gate[0], early_gate[1], early_out], axis=1)
    early_sum = seq_scatter(early_all, place)
    late = keep2.astype(F32) + flip_dp(send2, 1).astype(F32)
    late_a = fold(late[:, :, :SPLIT], bits[::-1])
    late_b = fold(late[:, :, SPLIT:], bits)
    late_sum = seq_scatter(jnp.concatenate([late_a, late_b], axis=1).reshape(size, shard_rows, WIDTH), place)
    raw_in = jnp.concatenate(
        [early_sum[:shard_rows], early_sum[shard_rows : 2 * shard_rows],
         late_sum[:, : in_weight.shape[1] - INNER]], axis=1
    )
    raw_out = early_sum[2 * shard_rows :]
    grad_norm_gain = jnp.sum(raw_in * in_weight.astype(F32), axis=1) / norm_gain.astype(F32)
    grad_gate_gain = jnp.sum(raw_out * out_weight.astype(F32), axis=1) / gate_gain.astype(F32)

    from_next = lax.ppermute(ghalo, BOTH, neighbour_pairs(-1))
    tail = (last + from_next).astype(BF16)
    gtok_second = jnp.concatenate([gtok[block_len : length - HALO], tail])
    grad_tokens = jnp.stack(from_stretch(gtok[:block_len], gtok_second, place))

    sums = sum_everywhere(small)
    grad_skip = jnp.sum(sums[6, :INNER].reshape(HEADS, HDIM), axis=1)
    return (
        outputs[:, None],
        grad_tokens[:, None],
        raw_in,
        raw_out,
        grad_norm_gain,
        grad_gate_gain,
        sums[0:KCONV, :CHANNELS],
        sums[4, :CHANNELS],
        sums[5, :HEADS],
        sums[5, LANES : LANES + HEADS],
        grad_skip,
    )


def solution(mesh):
    in_specs = (
        P(None, "dp", "seq", None),
        P(None, "dp"),
        P(None, "dp"),
        P(None, "dp", "seq", None),
        P(BOTH, None),
        P(BOTH, None),
        P(BOTH),
        P(BOTH),
        P(),
        P(),
        P(),
        P(),
        P(),
    )
    out_specs = (
        P(None, "dp", "seq", None),
        P(None, "dp", "seq", None),
        P(BOTH, None),
        P(BOTH, None),
        P(BOTH),
        P(BOTH),
        P(),
        P(),
        P(),
        P(),
        P(),
    )
    return jax.shard_map(per_device, mesh=mesh, in_specs=in_specs, out_specs=out_specs, check_vma=False)
```

time: 852 us -> 402 us (0.47)
  waiting for transfers between devices: 309 us -> 119 us
  local copies, waits for them, and re-layouts: 145 us -> 14.6 us
  Pallas kernels: 0 us -> 108 us
  matrix products: 96.7 us -> 0 us
  other arithmetic: 120 us -> 26.2 us
  blocking collectives: 83.7 us -> 0 us
  between operations: 15.9 us -> 43.7 us
  starting transfers between devices: 67.8 us -> 83.5 us
    ppermute x52 -> x70, waiting for transfers between devices: 304 us -> 119 us  [the longest x44 102 us: flip_dp(): return lax.ppermute(value, 'dp', pairs)]
    pallas_call x0 -> x6, Pallas kernels: none -> 108 us  [the longest x5 106 us: call(): pl.pallas_call(body, out_shape=[jax.ShapeDtypeStruct(shape, kind) for sha...]
    dot_general x36 -> x0, matrix products: 96.7 us -> none  [the longest x2 10.6 us: backward_micro(): jnp.einsum('bthp,bshp->btsh', grad_core, values, preferred_element_type=W...]
    unnamed x2 -> x0, blocking collectives: 83.7 us -> none
    scatter-add x10 -> x0, local copies, waits for them, and re-layouts: 64.6 us -> none  [the longest x6 47 us: backward_micro(): grad_extended.at[:, offset:offset + block_len]]
    add x24 -> x17, other arithmetic: 36.1 us -> 3.67 us  [the longest x1 1.66 us: per_device(): late = keep2.astype(F32) + flip_dp(send2, 1).astype(F32)]
    reduce_sum x16 -> x3, other arithmetic: 30.7 us -> 2.29 us  [the longest x1 0.88 us: per_device(): jnp.sum(raw_in * in_weight.astype(F32), axis=1) / norm_gain.astype(F32)]
    another operation x36 -> x2, local copies, waits for them, and re-layouts: 28.2 us -> 1.44 us  [the longest x1 0.77 us: per_device(): grad_skip = jnp.sum(sums[6, :INNER].reshape(HEADS, HDIM), axis=1)]
  transfers between devices with their start and end apart: 56 -> 70, of which waited for: 31 -> 25; matrix products, arithmetic and copies ran while one was open for 22% -> 9% of each run, Pallas kernels for 0% -> 21%
where the time goes in v1:
time: 402 us; the launch traced here: 394 us
  waiting for transfers between devices  119 us (30%)
  Pallas kernels  108 us (27%)
  starting transfers between devices  83.5 us (21%)
  between operations  43.7 us (11%)
  other arithmetic  26.2 us (7%)
  local copies, waits for them, and re-layouts  14.6 us (4%)
    pallas_call x5, Pallas kernels, call(): pl.pallas_call(body, out_shape=[jax.ShapeDtypeStruct(shape, kind) for sha...  106 us
    ppermute x44, waiting for transfers between devices, flip_dp(): return lax.ppermute(value, 'dp', pairs)  102 us
    ppermute x44, starting transfers between devices, flip_dp(): return lax.ppermute(value, 'dp', pairs)  40.9 us
    ppermute x12, starting transfers between devices, shift_seq(): lax.ppermute(value, 'seq', [(i, (i + step) % size) for i in range(size)])  19.2 us
    ppermute x12, waiting for transfers between devices, shift_seq(): lax.ppermute(value, 'seq', [(i, (i + step) % size) for i in range(size)])  12 us
  transfers between devices with their start and end apart: 70, of which 25 were waited for; matrix products, arithmetic and copies ran while one was open for 9% of the time, Pallas kernels for 21%

profile of v1, /device:TPU:0, one launch (start us, length us, event | category | flops | bytes accessed | tf_op | source)
XLA Modules:
  0.0 394.1 jit_solution(17600139559280849972)
XLA Ops:
  3.4 5.1 %collective-permute-start.6 = (bf16[24,1920]{1,0:T(8,128)(2,1)S(1)}, bf16[24,1920]{1,0:T(8,128)(2,1)S(1)}, u32[]{:S(2)}, u32[]{:S(2)}) collective-permute-start(bf16[24,1920]{1,0:T(8,128)(2,1)S(1)} %pad.22), channel_id=1, source_target_pairs={{0,3},{1,0},{2,1},{3,2},{4,7},{5,4},{6,5},{7,6},{8,11},{9,8},{10,9... | collective-permute-start | bytes 276488 | tf_op jit(solution)/shard_map/ppermute | solution.py:35
  57.1 9.9 %collective-permute-done.26 = bf16[2,128,768]{2,1,0:T(8,128)(2,1)S(1)} collective-permute-done((bf16[2,128,768]{2,1,0:T(8,128)(2,1)S(1)}, bf16[2,128,768]{2,1,0:T(8,128)(2,1)S(1)}, u32[]{:S(2)}, u32[]{:S(2)}) %collective-permute-start.26) | collective-permute-done | bytes 393248 | tf_op jit(solution)/shard_map/ppermute | solution.py:30
  71.6 12.8 %collective-permute-done.27 = bf16[2,128,768]{2,1,0:T(8,128)(2,1)S(1)} collective-permute-done((bf16[2,128,768]{2,1,0:T(8,128)(2,1)S(1)}, bf16[2,128,768]{2,1,0:T(8,128)(2,1)S(1)}, u32[]{:S(2)}, u32[]{:S(2)}) %collective-permute-start.27) | collective-permute-done | bytes 393248 | tf_op jit(solution)/shard_map/ppermute | solution.py:30
  87.6 9.1 %collective-permute-done.28 = bf16[2,128,768]{2,1,0:T(8,128)(2,1)S(1)} collective-permute-done((bf16[2,128,768]{2,1,0:T(8,128)(2,1)S(1)}, bf16[2,128,768]{2,1,0:T(8,128)(2,1)S(1)}, u32[]{:S(2)}, u32[]{:S(2)}) %collective-permute-start.28) | collective-permute-done | bytes 393248 | tf_op jit(solution)/shard_map/ppermute | solution.py:30
  101.3 11.2 %collective-permute-done.29 = bf16[2,128,768]{2,1,0:T(8,128)(2,1)S(1)} collective-permute-done((bf16[2,128,768]{2,1,0:T(8,128)(2,1)S(1)}, bf16[2,128,768]{2,1,0:T(8,128)(2,1)S(1)}, u32[]{:S(2)}, u32[]{:S(2)}) %collective-permute-start.29) | collective-permute-done | bytes 393248 | tf_op jit(solution)/shard_map/ppermute | solution.py:30
  118.9 12.2 %collective-permute-done.21.refs_1_ = bf16[2,192,768]{2,1,0:T(8,128)(2,1)S(1)} collective-permute-done((bf16[2,192,768]{2,1,0:T(8,128)(2,1)S(1)}, bf16[2,192,768]{2,1,0:T(8,128)(2,1)S(1)}, u32[]{:S(2)}, u32[]{:S(2)}) %collective-permute-start.21) | collective-permute-done | bytes 589856 | tf_op jit(solution)/shard_map/ppermute | solution.py:30
  141.8 16.6 %shard_map.213 = (bf16[528,768]{1,0:T(8,128)(2,1)}, bf16[528,1792]{1,0:T(8,128)(2,1)}, bf16[512,1792]{1,0:T(8,128)(2,1)}, f32[512,128]{1,0:T(8,128)}, f32[512,12...) custom-call(s32[2]{0:T(128)} %pad_add_fusion.4.scal, ...), custom_call_target="tpu_custom_call" | custom-call | tf_op jit(solution)/shard_map/pallas_call | solution.py:801
  161.1 9.4 %shard_map.214 = (f32[512,1536]{1,0:T(8,128)}, f32[512,1536]{1,0:T(8,128)}) custom-call(s32[2]{0:T(128)} %pad_add_fusion.4.scal, bf16[528,768]{1,0:T(8,128)(2,1)} %get-tuple-element.39.nh_ref, bf16[512,1792]{1,0:T(8,128)(2,1)} %get-tuple-element.40.act_ref, f32[512,128]{1,0:T(8,128)} %get-tuple-element.41.step_ref, f32[512,128]{1,0:T(8,128)} %get-tuple-element.42.cum_ref, ...), custom_call_target="tpu_custom_call" | custom-call | tf_op jit(solution)/shard_map/pallas_call | solution.py:801
  173.5 23.1 %shard_map.215 = (bf16[512,768]{1,0:T(8,128)(2,1)}, bf16[512,1536]{1,0:T(8,128)(2,1)}, bf16[512,1536]{1,0:T(8,128)(2,1)}, bf16[512,1536]{1,0:T(8,128)(2,1)}, f32...) custom-call(s32[2]{0:T(128)} %pad_add_fusion.4.scal, ...), custom_call_target="tpu_custom_call" | custom-call | tf_op jit(solution)/shard_map/pallas_call | solution.py:801
  202.9 20.1 %shard_map.216 = (f32[512,1536]{1,0:T(8,128)}, f32[512,256]{1,0:T(8,128)}, f32[512,768]{1,0:T(8,128)}, bf16[4,384,768]{2,1,0:T(8,128)(2,1)}, bf16[4,384,768]{2,1,0:T(8,128)(2,1)}) custom-call(s32[2]{0:T(128)} %pad_add_fusion.4.scal, bf16[512,1792]{1,0:T(8,128)(2,1)} %get-tuple-element.40.act_ref, f32[512,128]{1,0:T(8,128)} %get-tuple-element.41.step_ref, ...), custom_call_target="tpu_custom_call" | custom-call | tf_op jit(solution)/shard_map/pallas_call | solution.py:801
  223.8 36.7 %shard_map.217 = (bf16[512,768]{1,0:T(8,128)(2,1)}, f32[16,768]{1,0:T(8,128)}, f32[16,768]{1,0:T(8,128)}, bf16[4,96,1920]{2,1,0:T(8,128)(2,1)}, bf16[4,96,1920]{2,1,0:T(8,128)(2,1)}, /*index=5*/f32[8,1920]{1,0:T(8,128)}) custom-call(s32[2]{0:T(128)} %pad_add_fusion.4.scal, bf16[512,1792]{1,0:T(8,128)(2,1)} %get-tuple-element.40.act_ref, ...), custom_call_target="tpu_custom_call" | custom-call | tf_op jit(solution)/shard_map/pallas_call | solution.py:801
  286.2 3.1 collective-permute-done.66
  294.7 3.3 collective-permute-done.68
  303.4 4.5 %collective-permute-start.48 = (bf16[256,768]{1,0:T(8,128)(2,1)}, bf16[256,768]{1,0:T(8,128)(2,1)}, u32[]{:S(2)}, u32[]{:S(2)}) collective-permute-start(bf16[256,768]{1,0:T(8,128)(2,1)} %get-tuple-element.97), channel_id=1, source_target_pairs={{0,0},{2,1},{4,2},{6,3},{1,4},{3,5},{5,6},{7,7},{8,8},{10,9},{12,1... | collective-permute-start | bytes 1179656 | tf_op jit(solution)/shard_map/ppermute | solution.py:80
  313.0 6.8 %collective-permute-done.40 = bf16[2,128,768]{2,1,0:T(8,128)(2,1)S(1)} collective-permute-done((bf16[2,128,768]{2,1,0:T(8,128)(2,1)}, bf16[2,128,768]{2,1,0:T(8,128)(2,1)S(1)}, u32[]{:S(2)}, u32[]{:S(2)}) %collective-permute-start.40) | collective-permute-done | bytes 393248 | tf_op jit(solution)/shard_map/ppermute | solution.py:30
  323.6 6.4 %collective-permute-done.41 = bf16[2,128,768]{2,1,0:T(8,128)(2,1)S(1)} collective-permute-done((bf16[2,128,768]{2,1,0:T(8,128)(2,1)S(1)}, bf16[2,128,768]{2,1,0:T(8,128)(2,1)S(1)}, u32[]{:S(2)}, u32[]{:S(2)}) %collective-permute-start.41) | collective-permute-done | bytes 393248 | tf_op jit(solution)/shard_map/ppermute | solution.py:30
  335.4 6.7 %collective-permute-done.42 = bf16[2,128,768]{2,1,0:T(8,128)(2,1)S(1)} collective-permute-done((bf16[2,128,768]{2,1,0:T(8,128)(2,1)S(1)}, bf16[2,128,768]{2,1,0:T(8,128)(2,1)S(1)}, u32[]{:S(2)}, u32[]{:S(2)}) %collective-permute-start.42) | collective-permute-done | bytes 393248 | tf_op jit(solution)/shard_map/ppermute | solution.py:30
  345.2 4.4 %collective-permute-done.58 = bf16[2,96,1024]{2,1,0:T(8,128)(2,1)S(1)} collective-permute-done((bf16[2,96,1024]{2,1,0:T(8,128)(2,1)S(1)}, bf16[2,96,1024]{2,1,0:T(8,128)(2,1)S(1)}, u32[]{:S(2)}, u32[]{:S(2)}) %collective-permute-start.58) | collective-permute-done | bytes 393248 | tf_op jit(solution)/shard_map/ppermute | solution.py:30
  354.5 3.1 collective-permute-done.59
  357.9 3.1 collective-permute-start.63
  361.0 5.9 %collective-permute-done.52 = bf16[2,192,768]{2,1,0:T(8,128)(2,1)S(1)} collective-permute-done((bf16[2,192,768]{2,1,0:T(8,128)(2,1)S(1)}, bf16[2,192,768]{2,1,0:T(8,128)(2,1)S(1)}, u32[]{:S(2)}, u32[]{:S(2)}) %collective-permute-start.52) | collective-permute-done | bytes 589856 | tf_op jit(solution)/shard_map/ppermute | solution.py:30
  369.4 3.8 collective-permute-done.62
  375.9 3.9 collective-permute-start.56
  385.6 5.2 %collective-permute-done.55 = bf16[96,768]{1,0:T(8,128)(2,1)S(1)} collective-permute-done((bf16[96,768]{1,0:T(8,128)(2,1)S(1)}, bf16[96,768]{1,0:T(8,128)(2,1)S(1)}, u32[]{:S(2)}, u32[]{:S(2)}) %collective-permute-start.55) | collective-permute-done | bytes 147488 | tf_op jit(solution)/shard_map/ppermute | solution.py:35
  (318 shorter events, 124.0 us)
Async XLA Ops:
  3.4 46.4 %collective-permute-start.6 = (bf16[24,1920]{1,0:T(8,128)(2,1)S(1)}, bf16[24,1920]{1,0:T(8,128)(2,1)S(1)}, u32[]{:S(2)}, u32[]{:S(2)}) collective-permute-start(bf16[24,1920]{1,0:T(8,128)(2,1)S(1)} %pad.22), channel_id=1, source_target_pairs={{0,3},{1,0},{2,1},{3,2},{4,7},{5,4},{6,5},{7,6},{8,11},{9,8},{10,9... | collective-permute-start | bytes 276488 | tf_op jit(solution)/shard_map/ppermute | solution.py:35
  8.5 41.4 %collective-permute-start.7 = (bf16[24,1920]{1,0:T(8,128)(2,1)S(1)}, bf16[24,1920]{1,0:T(8,128)(2,1)S(1)}, u32[]{:S(2)}, u32[]{:S(2)}) collective-permute-start(bf16[24,1920]{1,0:T(8,128)(2,1)S(1)} %pad.22), channel_id=1, source_target_pairs={{0,2},{1,3},{2,0},{3,1},{4,6},{5,7},{6,4},{7,5},{8,10},{9,11},{10,... | collective-permute-start | bytes 276488 | tf_op jit(solution)/shard_map/ppermute | solution.py:35
  8.5 43.2 %collective-permute-start.8 = (bf16[24,1920]{1,0:T(8,128)(2,1)S(1)}, bf16[24,1920]{1,0:T(8,128)(2,1)S(1)}, u32[]{:S(2)}, u32[]{:S(2)}) collective-permute-start(bf16[24,1920]{1,0:T(8,128)(2,1)S(1)} %pad.22), channel_id=1, source_target_pairs={{0,1},{1,2},{2,3},{3,0},{4,5},{5,6},{6,7},{7,4},{8,9},{9,10},{10,1... | collective-permute-start | bytes 276488 | tf_op jit(solution)/shard_map/ppermute | solution.py:35
  12.6 55.1 %collective-permute-start.17 = (bf16[96,768]{1,0:T(8,128)(2,1)}, bf16[96,768]{1,0:T(8,128)(2,1)S(1)}, u32[]{:S(2)}, u32[]{:S(2)}) collective-permute-start(bf16[96,768]{1,0:T(8,128)(2,1)} %pad_maximum_fusion.26), channel_id=1, source_target_pairs={{0,3},{1,0},{2,1},{3,2},{4,7},{5,4},{6,5},{7,6},{8,11},{9,8},{10,9... | collective-permute-start | bytes 442376 | tf_op jit(solution)/shard_map/ppermute | solution.py:35
  24.2 45.1 %collective-permute-start.18 = (bf16[96,768]{1,0:T(8,128)(2,1)}, bf16[96,768]{1,0:T(8,128)(2,1)S(1)}, u32[]{:S(2)}, u32[]{:S(2)}) collective-permute-start(bf16[96,768]{1,0:T(8,128)(2,1)} %pad_maximum_fusion.26), channel_id=1, source_target_pairs={{0,2},{1,3},{2,0},{3,1},{4,6},{5,7},{6,4},{7,5},{8,10},{9,11},{10,... | collective-permute-start | bytes 442376 | tf_op jit(solution)/shard_map/ppermute | solution.py:35
  49.8 21.0 %collective-permute-start.19 = (bf16[96,768]{1,0:T(8,128)(2,1)}, bf16[96,768]{1,0:T(8,128)(2,1)S(1)}, u32[]{:S(2)}, u32[]{:S(2)}) collective-permute-start(bf16[96,768]{1,0:T(8,128)(2,1)} %pad_maximum_fusion.26), channel_id=1, source_target_pairs={{0,1},{1,2},{2,3},{3,0},{4,5},{5,6},{6,7},{7,4},{8,9},{9,10},{10,1... | collective-permute-start | bytes 442376 | tf_op jit(solution)/shard_map/ppermute | solution.py:35
  49.9 47.4 %collective-permute-start.4 = (bf16[256,768]{1,0:T(8,128)(2,1)S(1)}, bf16[256,768]{1,0:T(8,128)(2,1)S(1)}, u32[]{:S(2)}, u32[]{:S(2)}) collective-permute-start(bf16[256,768]{1,0:T(8,128)(2,1)S(1)} %get-tuple-element.126), channel_id=1, source_target_pairs={{0,2},{1,0},{2,6},{3,4},{4,3},{5,1},{6,7},{7,5},{8,10},{9,8},{10,1... | collective-permute-start | bytes 1179656 | tf_op jit(solution)/shard_map/ppermute | solution.py:73
  66.9 32.0 %collective-permute-start.3 = (bf16[256,768]{1,0:T(8,128)(2,1)S(1)}, bf16[256,768]{1,0:T(8,128)(2,1)S(1)}, u32[]{:S(2)}, u32[]{:S(2)}) collective-permute-start(bf16[256,768]{1,0:T(8,128)(2,1)S(1)} %get-tuple-element.127), channel_id=1, source_target_pairs={{0,0},{1,2},{2,4},{3,6},{4,1},{5,3},{6,5},{7,7},{8,8},{9,10},{10,1... | collective-permute-start | bytes 1179656 | tf_op jit(solution)/shard_map/ppermute | solution.py:72
  86.3 28.7 %collective-permute-start.20 = (bf16[1,192,768]{2,1,0:T(8,128)(2,1)S(1)}, bf16[1,192,768]{2,1,0:T(8,128)(2,1)S(1)}, u32[]{:S(2)}, u32[]{:S(2)}) collective-permute-start(bf16[1,192,768]{2,1,0:T(8,128)(2,1)S(1)} %bitcast.213), channel_id=1, source_target_pairs={{0,8},{4,12},{8,0},{12,4},{16,24},{20,28},{24,16},{28,20},{1,9},{5... | collective-permute-start | bytes 884744 | tf_op jit(solution)/shard_map/ppermute | solution.py:30
  87.0 28.3 %collective-permute-start.33 = (bf16[1,192,896]{2,1,0:T(8,128)(2,1)S(1)}, bf16[1,192,896]{2,1,0:T(8,128)(2,1)S(1)}, u32[]{:S(2)}, u32[]{:S(2)}) collective-permute-start(bf16[1,192,896]{2,1,0:T(8,128)(2,1)S(1)} %fusion.10), channel_id=1, source_target_pairs={{0,16},{4,20},{8,24},{12,28},{16,0},{20,4},{24,8},{28,12},{1,17},{... | collective-permute-start | bytes 1032200 | tf_op jit(solution)/shard_map/ppermute | solution.py:30
  97.3 20.1 %collective-permute-start.10 = (bf16[2,96,1024]{2,1,0:T(8,128)(2,1)S(1)}, bf16[2,96,1024]{2,1,0:T(8,128)(2,1)S(1)}, u32[]{:S(2)}, u32[]{:S(2)}) collective-permute-start(bf16[2,96,1024]{2,1,0:T(8,128)(2,1)S(1)} %pad_maximum_fusion.9.refs_0_), channel_id=1, source_target_pairs={{0,16},{4,20},{8,24},{12,28},{16,0},{20,4},{24,8},{28,12},{1,17},{... | collective-permute-start | bytes 1179656 | tf_op jit(solution)/shard_map/ppermute | solution.py:30
  131.1 27.3 %collective-permute-start.23 = (bf16[2,192,768]{2,1,0:T(8,128)(2,1)S(1)}, bf16[2,192,768]{2,1,0:T(8,128)(2,1)S(1)}, u32[]{:S(2)}, u32[]{:S(2)}) collective-permute-start(bf16[2,192,768]{2,1,0:T(8,128)(2,1)S(1)} %collective-permute-done.21.refs_1_), channel_id=1, source_target_pairs={{0,4},{4,0},{8,12},{12,8},{16,20},{20,16},{24,28},{28,24},{1,5},{5... | collective-permute-start | bytes 1769480 | tf_op jit(solution)/shard_map/ppermute | solution.py:30
  132.1 38.5 %collective-permute-start.31 = (bf16[256,768]{1,0:T(8,128)(2,1)}, bf16[256,768]{1,0:T(8,128)(2,1)}, u32[]{:S(2)}, u32[]{:S(2)}) collective-permute-start(bf16[256,768]{1,0:T(8,128)(2,1)} %get-tuple-element.118), channel_id=1, source_target_pairs={{0,2},{1,0},{2,6},{3,4},{4,3},{5,1},{6,7},{7,5},{8,10},{9,8},{10,1... | collective-permute-start | bytes 1179656 | tf_op jit(solution)/shard_map/ppermute | solution.py:73
  132.2 38.4 %collective-permute-start.32 = (bf16[256,768]{1,0:T(8,128)(2,1)S(1)}, bf16[256,768]{1,0:T(8,128)(2,1)}, u32[]{:S(2)}, u32[]{:S(2)}) collective-permute-start(bf16[256,768]{1,0:T(8,128)(2,1)S(1)} %get-tuple-element.119), channel_id=1, source_target_pairs={{0,0},{1,2},{2,4},{3,6},{4,1},{5,3},{6,5},{7,7},{8,8},{9,10},{10,1... | collective-permute-start | bytes 1179656 | tf_op jit(solution)/shard_map/ppermute | solution.py:72
  134.1 38.6 %collective-permute-start.35 = (bf16[2,192,896]{2,1,0:T(8,128)(2,1)S(1)}, bf16[2,192,896]{2,1,0:T(8,128)(2,1)}, u32[]{:S(2)}, u32[]{:S(2)}) collective-permute-start(bf16[2,192,896]{2,1,0:T(8,128)(2,1)S(1)} %pad_maximum_fusion.4.refs_0_), channel_id=1, source_target_pairs={{0,4},{4,0},{8,12},{12,8},{16,20},{20,16},{24,28},{28,24},{1,5},{5... | collective-permute-start | bytes 2064392 | tf_op jit(solution)/shard_map/ppermute | solution.py:30
  136.8 35.9 %collective-permute-start.36 = (bf16[2,192,896]{2,1,0:T(8,128)(2,1)}, bf16[2,192,896]{2,1,0:T(8,128)(2,1)}, u32[]{:S(2)}, u32[]{:S(2)}) collective-permute-start(bf16[2,192,896]{2,1,0:T(8,128)(2,1)} %collective-permute-done.34.refs_1_), channel_id=1, source_target_pairs={{0,4},{4,0},{8,12},{12,8},{16,20},{20,16},{24,28},{28,24},{1,5},{5... | collective-permute-start | bytes 2064392 | tf_op jit(solution)/shard_map/ppermute | solution.py:30
  196.5 26.5 %collective-permute-start.45 = (bf16[128,1536]{1,0:T(8,128)(2,1)}, bf16[128,1536]{1,0:T(8,128)(2,1)S(1)}, u32[]{:S(2)}, u32[]{:S(2)}) collective-permute-start(bf16[128,1536]{1,0:T(8,128)(2,1)} %get-tuple-element.56), channel_id=1, source_target_pairs={{4,0},{5,1},{6,2},{7,3},{12,8},{13,9},{14,10},{15,11},{20,16},{21,... | collective-permute-start | bytes 1179656 | tf_op jit(solution)/shard_map/ppermute | solution.py:902
  199.0 86.1 %collective-permute-start.37 = (bf16[256,768]{1,0:T(8,128)(2,1)S(1)}, bf16[256,768]{1,0:T(8,128)(2,1)S(1)}, u32[]{:S(2)}, u32[]{:S(2)}) collective-permute-start(bf16[256,768]{1,0:T(8,128)(2,1)S(1)} %get-tuple-element.114), channel_id=1, source_target_pairs={{2,0},{0,1},{6,2},{4,3},{3,4},{1,5},{7,6},{5,7},{10,8},{8,9},{14,1... | collective-permute-start | bytes 1179656 | tf_op jit(solution)/shard_map/ppermute | solution.py:81
  201.5 83.7 %collective-permute-start.38 = (bf16[256,768]{1,0:T(8,128)(2,1)S(1)}, bf16[256,768]{1,0:T(8,128)(2,1)}, u32[]{:S(2)}, u32[]{:S(2)}) collective-permute-start(bf16[256,768]{1,0:T(8,128)(2,1)S(1)} %get-tuple-element.115), channel_id=1, source_target_pairs={{0,0},{2,1},{4,2},{6,3},{1,4},{3,5},{5,6},{7,7},{8,8},{10,9},{12,1... | collective-permute-start | bytes 1179656 | tf_op jit(solution)/shard_map/ppermute | solution.py:80
  260.5 23.2 %collective-permute-start.65 = (f32[8,1920]{1,0:T(8,128)}, f32[8,1920]{1,0:T(8,128)}, u32[]{:S(2)}, u32[]{:S(2)}) collective-permute-start(f32[8,1920]{1,0:T(8,128)} %get-tuple-element.66), channel_id=1, source_target_pairs={{0,4},{4,0},{8,12},{12,8},{16,20},{20,16},{24,28},{28,24},{1,5},{5... | collective-permute-start | bytes 184328 | tf_op jit(solution)/shard_map/ppermute | solution.py:30
  282.2 68.1 %collective-permute-start.49 = (bf16[4,384,768]{2,1,0:T(8,128)(2,1)}, bf16[4,384,768]{2,1,0:T(8,128)(2,1)S(1)}, u32[]{:S(2)}, u32[]{:S(2)}) collective-permute-start(bf16[4,384,768]{2,1,0:T(8,128)(2,1)} %get-tuple-element.63), channel_id=1, source_target_pairs={{0,4},{4,0},{8,12},{12,8},{16,20},{20,16},{24,28},{28,24},{1,5},{5... | collective-permute-start | bytes 7077896 | tf_op jit(solution)/shard_map/ppermute | solution.py:30
  291.2 40.6 %collective-permute-start.57 = (bf16[4,96,1920]{2,1,0:T(8,128)(2,1)}, bf16[4,96,1920]{2,1,0:T(8,128)(2,1)}, u32[]{:S(2)}, u32[]{:S(2)}) collective-permute-start(bf16[4,96,1920]{2,1,0:T(8,128)(2,1)} %get-tuple-element.65), channel_id=1, source_target_pairs={{0,4},{4,0},{8,12},{12,8},{16,20},{20,16},{24,28},{28,24},{1,5},{5... | collective-permute-start | bytes 4423688 | tf_op jit(solution)/shard_map/ppermute | solution.py:30
  301.5 20.0 %collective-permute-start.47 = (bf16[256,768]{1,0:T(8,128)(2,1)}, bf16[256,768]{1,0:T(8,128)(2,1)}, u32[]{:S(2)}, u32[]{:S(2)}) collective-permute-start(bf16[256,768]{1,0:T(8,128)(2,1)} %get-tuple-element.96), channel_id=1, source_target_pairs={{2,0},{0,1},{6,2},{4,3},{3,4},{1,5},{7,6},{5,7},{10,8},{8,9},{14,1... | collective-permute-start | bytes 1179656 | tf_op jit(solution)/shard_map/ppermute | solution.py:81
  354.3 27.4 %collective-permute-start.44 = (bf16[2,128,768]{2,1,0:T(8,128)(2,1)S(1)}, bf16[2,128,768]{2,1,0:T(8,128)(2,1)S(1)}, u32[]{:S(2)}, u32[]{:S(2)}) collective-permute-start(bf16[2,128,768]{2,1,0:T(8,128)(2,1)S(1)} %pad_maximum_fusion.21), channel_id=1, source_target_pairs={{0,4},{4,0},{8,12},{12,8},{16,20},{20,16},{24,28},{28,24},{1,5},{5... | collective-permute-start | bytes 1179656 | tf_op jit(solution)/shard_map/ppermute | solution.py:30
  (80 other events, 877.6 us)
